TPU v7x, 32 devices: a whole 2x2x4 slice. The times are simulated.
32 devices in a mesh: fsdp: 2 (over x), ctx: 4 (over z), tp: 4 (over y, core).
Axes of the slice: x: 2, y: 2, z: 4, core: 2. Of those that a mesh axis runs over, the one named last changes fastest.
Arguments:
- tokens: bfloat16 [4, 1024, 2048], P('fsdp', 'ctx'), may hold values from -36 to 36
- cotangent: bfloat16 [4, 1024, 2048], P('fsdp', 'ctx'), may hold values from -9 to 9
- lengths: int32 [4, 2], P('fsdp'), may hold values from 1 to 768, 1024 in all within a row
- deal: int32 [4, 1024], P('fsdp'), may hold values from 0 to 1023, each once within a row
- att_proj: float32 [3, 2048, 2048], P(None, ('fsdp', 'ctx'), 'tp'), may hold values from -0.125 to 0.125
- attn_out: float32 [2048, 2048], P(('fsdp', 'ctx'), 'tp'), may hold values from -0.75 to 0.75
- ff_proj: float32 [2, 2048, 8192], P(None, ('fsdp', 'ctx'), 'tp'), may hold values from -0.125 to 0.125
- ff_out: float32 [2048, 8192], P(('fsdp', 'ctx'), 'tp'), may hold values from -0.0625 to 0.0625
- att_proj_first: float32 [3, 2048, 2048], P(None, ('fsdp', 'ctx'), 'tp')
- attn_out_first: float32 [2048, 2048], P(('fsdp', 'ctx'), 'tp')
- ff_proj_first: float32 [2, 2048, 8192], P(None, ('fsdp', 'ctx'), 'tp')
- ff_out_first: float32 [2048, 8192], P(('fsdp', 'ctx'), 'tp')
- att_proj_second: float32 [3, 2048, 2048], P(None, ('fsdp', 'ctx'), 'tp'), as said below
- attn_out_second: float32 [2048, 2048], P(('fsdp', 'ctx'), 'tp'), as said below
- ff_proj_second: float32 [2, 2048, 8192], P(None, ('fsdp', 'ctx'), 'tp'), as said below
- ff_out_second: float32 [2048, 8192], P(('fsdp', 'ctx'), 'tp'), as said below
Outputs:
- block_out: bfloat16 [4, 1024, 2048], P('fsdp', 'ctx')
- input_grad: float32 [4, 1024, 2048], P('fsdp', 'ctx')
- grad_norm: float32 [1], replicated
- att_proj_grad: float32 [3, 2048, 2048], P(None, ('fsdp', 'ctx'), 'tp')
- attn_out_grad: float32 [2048, 2048], P(('fsdp', 'ctx'), 'tp')
- ff_proj_grad: float32 [2, 2048, 8192], P(None, ('fsdp', 'ctx'), 'tp')
- ff_out_grad: float32 [2048, 8192], P(('fsdp', 'ctx'), 'tp')
- att_proj_first_new: float32 [3, 2048, 2048], P(None, ('fsdp', 'ctx'), 'tp')
- attn_out_first_new: float32 [2048, 2048], P(('fsdp', 'ctx'), 'tp')
- ff_proj_first_new: float32 [2, 2048, 8192], P(None, ('fsdp', 'ctx'), 'tp')
- ff_out_first_new: float32 [2048, 8192], P(('fsdp', 'ctx'), 'tp')
- att_proj_second_new: float32 [3, 2048, 2048], P(None, ('fsdp', 'ctx'), 'tp')
- attn_out_second_new: float32 [2048, 2048], P(('fsdp', 'ctx'), 'tp')
- ff_proj_second_new: float32 [2, 2048, 8192], P(None, ('fsdp', 'ctx'), 'tp')
- ff_out_second_new: float32 [2048, 8192], P(('fsdp', 'ctx'), 'tp')
- att_proj_new: float32 [3, 2048, 2048], P(None, ('fsdp', 'ctx'), 'tp')
- attn_out_new: float32 [2048, 2048], P(('fsdp', 'ctx'), 'tp')
- ff_proj_new: float32 [2, 2048, 8192], P(None, ('fsdp', 'ctx'), 'tp')
- ff_out_new: float32 [2048, 8192], P(('fsdp', 'ctx'), 'tp')
- att_proj_low: bfloat16 [3, 2048, 2048], P(None, ('fsdp', 'ctx'), 'tp')
- attn_out_low: bfloat16 [2048, 2048], P(('fsdp', 'ctx'), 'tp')
- ff_proj_low: bfloat16 [2, 2048, 8192], P(None, ('fsdp', 'ctx'), 'tp')
- ff_out_low: bfloat16 [2048, 8192], P(('fsdp', 'ctx'), 'tp')
Inputs may be any that keep to these rules, and one draw needn't show every extreme that they name: `lengths`: each row sums to 1024 and no entry exceeds 768. `deal`: each row is a permutation of the positions of its pack. `att_proj_second`: every entry is positive. `attn_out_second`: every entry is positive. `ff_proj_second`: every entry is positive. `ff_out_second`: every entry is positive.
All inputs are finite; a program needn't handle non-finite values.
Results may differ from a plain program's by a relative error of at most 0.017.
Values may be sent and summed in bfloat16 or wider, within the bound.
A program may use at most 320 MiB of HBM per device.

v0:
```python
import jax
import jax.numpy as jnp
from jax import lax
from jax.sharding import PartitionSpec as P

HEAD_DIM = 128
STEP = 10
EPS_NORM = 1e-05
BETA_ONE = 0.9
BETA_TWO = 0.95
EPS_ADAM = 1e-08
DECAY = 0.1
MAX_NORM = 1.0
NEG_FILL = -1e30
BF = jnp.bfloat16
F32 = jnp.float32


def mean_spread(values):
    centre = values - jnp.mean(values, axis=-1, keepdims=True)
    spread = jnp.mean(centre * centre, axis=-1, keepdims=True)
    scale = lax.rsqrt(spread + EPS_NORM)
    return (centre * scale, scale)


def norm_back(grad, normed, scale):
    return scale * (
        grad
        - jnp.mean(grad, axis=-1, keepdims=True)
        - normed * jnp.mean(grad * normed, axis=-1, keepdims=True)
    )


def dot(left, right, dims):
    return lax.dot_general(left, right, (dims, ((), ())), preferred_element_type=F32)


def adam_step(weight, grad_sum, first, second, clip_factor, learn_rate):
    clipped = grad_sum * clip_factor
    first_new = BETA_ONE * first + (1.0 - BETA_ONE) * clipped
    second_new = BETA_TWO * second + (1.0 - BETA_TWO) * clipped * clipped
    first_hat = first_new / (1.0 - BETA_ONE**STEP)
    second_hat = second_new / (1.0 - BETA_TWO**STEP)
    weight_new = weight - learn_rate * (
        first_hat / (jnp.sqrt(second_hat) + EPS_ADAM) + DECAY * weight
    )
    return (first_new, second_new, weight_new)


def make_shards(mesh):
    n_f, n_c, n_t = (mesh.shape[a] for a in ("fsdp", "ctx", "tp"))

    def by_ctx(block, shift):
        return lax.ppermute(block, "ctx", [(i, (i + shift) % n_c) for i in range(n_c)])

    def by_core(block):
        return lax.ppermute(block, "tp", [(i, i ^ 1) for i in range(n_t)])

    def by_pack(block, shift, other):
        pairs = [
            (f * n_t + t, (f + shift) % n_f * n_t + (t ^ 2 * other))
            for f in range(n_f)
            for t in range(n_t)
        ]
        return lax.ppermute(block, ("fsdp", "tp"), pairs)

    def gather_rows(half):
        mine = jnp.stack([half] + [by_ctx(half, s) for s in range(1, n_c)])
        both = jnp.stack([mine, by_core(mine)], axis=1)
        return both.reshape(-1, half.shape[1])

    def scatter_rows(partial):
        width = partial.shape[1]
        split = partial.astype(BF).reshape(n_c, 2, -1, width)
        summed = split[:, 0].astype(F32) + by_core(split[:, 1]).astype(F32)
        sent = summed.astype(BF)
        total = summed[0]
        for j in range(1, n_c):
            total = total + by_ctx(sent[j], -j).astype(F32)
        return total

    def gather_weight(shard):
        swapped = lax.all_to_all(shard.astype(BF), "ctx", 2, 1, tiled=True)
        columns = []
        for other in range(2):
            parts = [
                swapped if s == 0 and other == 0 else by_pack(swapped, s, other) for s in range(n_f)
            ]
            columns.append(jnp.concatenate(parts, axis=1))
        return jnp.concatenate(columns, axis=2)

    def scatter_grad(grad):
        count, height, width = grad.shape
        low = grad.astype(BF).reshape(count, n_f, height // n_f, 2, width // 2)
        total = grad.reshape(low.shape)[:, 0, :, 0]
        for other in range(2):
            for i in range(n_f):
                if i or other:
                    total = total + by_pack(low[:, i, :, other], -i, other).astype(F32)
        return lax.all_to_all(total.astype(BF), "ctx", 1, 2, tiled=True).astype(F32)

    def shards(
        tokens,
        cotangent,
        lengths,
        deal,
        att_proj,
        attn_out,
        ff_proj,
        ff_out,
        att_proj_first,
        attn_out_first,
        ff_proj_first,
        ff_out_first,
        att_proj_second,
        attn_out_second,
        ff_proj_second,
        ff_out_second,
    ):
        f_at, c_at, t_at = (lax.axis_index(a) for a in ("fsdp", "ctx", "tp"))
        pack_at, core_at = (t_at // 2, t_at % 2)
        packs, row_count, width = tokens.shape
        half = row_count // 2
        pack_len = deal.shape[1]
        score_scale = HEAD_DIM ** (-0.5)
        f_width = width // n_f

        def turned(rows):
            return jnp.concatenate(
                [
                    lax.dynamic_slice_in_dim(rows, (f_at - i) % n_f * f_width, f_width, 1)
                    for i in range(n_f)
                ],
                axis=1,
            )

        def own_rows(array):
            rows = array.reshape(packs * 2, half, width)
            return turned(lax.dynamic_index_in_dim(rows, t_at, 0, keepdims=False))

        own_tokens = own_rows(tokens)
        own_cot = own_rows(cotangent)
        att_w = gather_weight(jnp.concatenate([att_proj, attn_out[None]]))
        own_input = own_tokens.astype(F32)
        normed_one, scale_one = mean_spread(own_input)
        act_one = gather_rows(normed_one.astype(BF))
        deal_pack = lax.dynamic_index_in_dim(deal, pack_at, 0, keepdims=False)
        length_row = lax.dynamic_index_in_dim(lengths, pack_at, 0, keepdims=False)
        places = jnp.concatenate(
            [
                lax.dynamic_slice_in_dim(
                    deal_pack, (c_at - j) % n_c * row_count + (core_at + h) % 2 * half, half
                )
                for j in range(n_c)
                for h in range(2)
            ]
        )
        seqs = lengths.shape[1]
        before = jnp.arange(seqs)[:, None] > jnp.arange(seqs)[None, :]
        starts = jnp.sum(jnp.where(before, length_row[None, :], 0), axis=1)
        inside = (places[:, None] >= starts[None, :]) & (
            places[:, None] < (starts + length_row)[None, :]
        )
        firsts = jnp.sum(jnp.where(inside, starts[None, :], 0), axis=1)
        allowed = (places[None, :] <= places[:, None]) & (places[None, :] >= firsts[:, None])
        freq_steps = jnp.arange(HEAD_DIM // 2, dtype=F32)
        inverse = jnp.power(10000.0, -2.0 * freq_steps / HEAD_DIM)
        angles = (places - firsts).astype(F32)[:, None] * inverse[None, :]
        cos_table, sine_table = (jnp.cos(angles), jnp.sin(angles))

        def turn(values, sign):
            low, high = (values[..., : HEAD_DIM // 2], values[..., HEAD_DIM // 2 :])
            sine = sign * sine_table[:, None, :]
            cos = cos_table[:, None, :]
            return jnp.concatenate([low * cos - high * sine, high * cos + low * sine], axis=-1)

        rank_width = att_w.shape[2]
        heads = rank_width // HEAD_DIM
        raw = [
            dot(act_one, att_w[i], ((1,), (0,))).reshape(pack_len, heads, HEAD_DIM)
            for i in range(3)
        ]
        query = turn(raw[0], 1.0).astype(BF)
        key = turn(raw[1], 1.0).astype(BF)
        value = raw[2].astype(BF)
        scores = jnp.einsum("thd,khd->htk", query, key, preferred_element_type=F32) * score_scale
        scores = jnp.where(allowed[None], scores, NEG_FILL)
        exp_scores = jnp.exp(scores - jnp.max(scores, axis=2, keepdims=True))
        probs = exp_scores / jnp.sum(exp_scores, axis=2, keepdims=True)
        probs_low = probs.astype(BF)
        attended = jnp.einsum("htk,khd->thd", probs_low, value, preferred_element_type=F32)
        attended_low = attended.reshape(pack_len, rank_width).astype(BF)
        out_part = dot(attended_low, att_w[3], ((1,), (1,)))
        resid_mid = own_input + scatter_rows(out_part)
        normed_two, scale_two = mean_spread(resid_mid)
        act_two = gather_rows(normed_two.astype(BF))
        ff_w = gather_weight(jnp.concatenate([ff_proj, ff_out[None]]))
        cot_rows = gather_rows(own_cot)
        up = dot(act_two, ff_w[0], ((1,), (0,)))
        gate = dot(act_two, ff_w[1], ((1,), (0,)))
        sigma = jax.nn.sigmoid(gate)
        hidden_low = (gate * sigma * up).astype(BF)
        hidden_grad = dot(cot_rows, ff_w[2], ((1,), (0,)))
        up_grad = (hidden_grad * gate * sigma).astype(BF)
        gate_grad = (hidden_grad * up * sigma * (1.0 + gate * (1.0 - sigma))).astype(BF)
        act_two_part = dot(up_grad, ff_w[0], ((1,), (1,))) + dot(gate_grad, ff_w[1], ((1,), (1,)))
        act_two_grad = scatter_rows(act_two_part)
        mid_grad = own_cot.astype(F32) + norm_back(act_two_grad, normed_two, scale_two)
        mid_rows = gather_rows(mid_grad.astype(BF))
        ff_branch = scatter_rows(dot(hidden_low, ff_w[2], ((1,), (1,))))
        block_rows = turned((resid_mid + ff_branch).astype(BF))
        block_out = lax.all_gather(block_rows, "tp", axis=0, tiled=True)
        ff_grad = jnp.stack(
            [
                dot(act_two, up_grad, ((0,), (0,))),
                dot(act_two, gate_grad, ((0,), (0,))),
                dot(cot_rows, hidden_low, ((0,), (0,))),
            ]
        )
        ff_total = scatter_grad(ff_grad)
        attended_grad = dot(mid_rows, att_w[3], ((1,), (0,))).astype(BF)
        attended_grad = attended_grad.reshape(pack_len, heads, HEAD_DIM)
        value_grad = jnp.einsum(
            "htk,thd->khd", probs_low, attended_grad, preferred_element_type=F32
        )
        prob_grad = jnp.einsum("thd,khd->htk", attended_grad, value, preferred_element_type=F32)
        delta_rows = jnp.sum(probs * prob_grad, axis=2, keepdims=True)
        score_grad = (probs * (prob_grad - delta_rows)).astype(BF)
        query_grad = (
            jnp.einsum("htk,khd->thd", score_grad, key, preferred_element_type=F32) * score_scale
        )
        key_grad = (
            jnp.einsum("htk,thd->khd", score_grad, query, preferred_element_type=F32) * score_scale
        )
        joint_grad = [
            part.reshape(pack_len, rank_width).astype(BF)
            for part in (turn(query_grad, -1.0), turn(key_grad, -1.0), value_grad)
        ]
        act_one_part = sum((dot(joint_grad[i], att_w[i], ((1,), (1,))) for i in range(3)))
        act_one_grad = scatter_rows(act_one_part)
        input_rows = turned(norm_back(act_one_grad, normed_one, scale_one) + mid_grad)
        input_grad = lax.all_gather(input_rows, "tp", axis=0, tiled=True)
        att_grad = jnp.stack(
            [dot(act_one, part, ((0,), (0,))) for part in joint_grad]
            + [dot(mid_rows, attended_low, ((0,), (0,)))]
        )
        att_total = scatter_grad(att_grad)
        square_sum = lax.psum(
            jnp.sum(att_total * att_total) + jnp.sum(ff_total * ff_total), ("fsdp", "ctx", "tp")
        )
        norm_value = jnp.sqrt(square_sum)
        clip_factor = jnp.minimum(1.0, MAX_NORM / (norm_value + 1e-06))
        base_rate = width ** (-0.5)
        out_rate = (width // 32) ** (-0.5)
        grads = (att_total[:3], att_total[3], ff_total[:2], ff_total[2])
        weights = (att_proj, attn_out, ff_proj, ff_out)
        firsts_old = (att_proj_first, attn_out_first, ff_proj_first, ff_out_first)
        seconds_old = (att_proj_second, attn_out_second, ff_proj_second, ff_out_second)
        rates = (base_rate, out_rate, base_rate, base_rate)
        news = [
            adam_step(w, g, m, v, clip_factor, r)
            for w, g, m, v, r in zip(weights, grads, firsts_old, seconds_old, rates)
        ]
        return (
            block_out.reshape(tokens.shape),
            input_grad.reshape(tokens.shape),
            norm_value.reshape(1),
            *grads,
            *(n[0] for n in news),
            *(n[1] for n in news),
            *(n[2] for n in news),
            *(n[2].astype(BF) for n in news),
        )

    return shards


def solution(mesh):
    act = P("fsdp", "ctx", None)
    table = P("fsdp", None)
    cube = P(None, ("fsdp", "ctx"), "tp")
    flat = P(("fsdp", "ctx"), "tp")
    group = (cube, flat, cube, flat)
    in_specs = (act, act, table, table) + group * 3
    out_specs = (act, act, P()) + group * 5
    return jax.shard_map(
        make_shards(mesh), mesh=mesh, in_specs=in_specs, out_specs=out_specs, check_vma=False
    )
```

profile of v0, /device:TPU:0, one launch (start us, length us, event | category | flops | bytes accessed | tf_op | source)
XLA Modules:
  0.0 1239.6 jit_solution(7783477940593059198)
XLA Ops:
  10.2 5.0 collective-permute-start.2
  23.6 4.4 collective-permute-done.2
  28.0 44.8 %collective-permute-done.1 = bf16[128,2048]{1,0:T(8,128)(2,1)} collective-permute-done((bf16[128,2048]{1,0:T(8,128)(2,1)}, bf16[128,2048]{1,0:T(8,128)(2,1)}, u32[]{:S(2)}, u32[]{:S(2)}) %collective-permute-start.1) | collective-permute-done | bytes 524320 | tf_op jit(solution)/shard_map/ppermute | solution.py:54
  77.3 5.4 all-to-all-done
  93.8 17.7 %collective-permute-done.6 = bf16[4,1024,128]{1,2,0:T(8,128)(2,1)S(1)} collective-permute-done((bf16[4,1024,128]{1,2,0:T(8,128)(2,1)S(1)}, bf16[4,1024,128]{1,2,0:T(8,128)(2,1)S(1)}, u32[]{:S(2)}, u32[]{:S(2)}) %collective-permute-start.6) | collective-permute-done | bytes 1048608 | tf_op jit(solution)/shard_map/ppermute | solution.py:65
  111.4 20.4 %collective-permute-done.5 = bf16[4,1024,128]{1,2,0:T(8,128)(2,1)S(1)} collective-permute-done((bf16[4,1024,128]{1,2,0:T(8,128)(2,1)S(1)}, bf16[4,1024,128]{1,2,0:T(8,128)(2,1)S(1)}, u32[]{:S(2)}, u32[]{:S(2)}) %collective-permute-start.5) | collective-permute-done | bytes 1048608 | tf_op jit(solution)/shard_map/ppermute | solution.py:65
  137.3 6.0 fusion.127
  157.8 6.8 copy.340
  164.7 7.1 pad_maximum_fusion.4
  171.8 5.3 all-to-all-start.1
  189.7 71.6 %collective-permute-done.10 = bf16[128,2048]{1,0:T(8,128)(2,1)S(1)} collective-permute-done((bf16[128,2048]{1,0:T(8,128)(2,1)S(1)}, bf16[128,2048]{1,0:T(8,128)(2,1)S(1)}, u32[]{:S(2)}, u32[]{:S(2)}) %collective-permute-start.10) | collective-permute-done | bytes 524320 | tf_op jit(solution)/shard_map/ppermute | solution.py:54
  261.3 65.1 %collective-permute-start.22 = (bf16[128,2048]{1,0:T(8,128)(2,1)S(1)}, bf16[128,2048]{1,0:T(8,128)(2,1)S(1)}, u32[]{:S(2)}, u32[]{:S(2)}) collective-permute-start(bf16[128,2048]{1,0:T(8,128)(2,1)S(1)} %get-tuple-element.108), channel_id=1, source_target_pairs={{0,4},{4,8},{8,12},{12,0},{1,5},{5,9},{9,13},{13,1},{2,6},{6,10},{... | collective-permute-start | bytes 1572872 | tf_op jit(solution)/shard_map/ppermute | solution.py:54
  329.5 12.8 %collective-permute-start.13 = (bf16[128,2048]{1,0:T(8,128)(2,1)}, bf16[128,2048]{1,0:T(8,128)(2,1)}, u32[]{:S(2)}, u32[]{:S(2)}) collective-permute-start(bf16[128,2048]{1,0:T(8,128)(2,1)} %fusion.76), channel_id=1, source_target_pairs={{0,12},{4,0},{8,4},{12,8},{1,13},{5,1},{9,5},{13,9},{2,14},{6,2},{... | collective-permute-start | bytes 1572872 | tf_op jit(solution)/shard_map/ppermute | solution.py:54
  342.8 8.0 collective-permute-start.11
  350.8 33.1 %collective-permute-done.23 = bf16[128,2048]{1,0:T(8,128)(2,1)S(1)} collective-permute-done((bf16[128,2048]{1,0:T(8,128)(2,1)S(1)}, bf16[128,2048]{1,0:T(8,128)(2,1)S(1)}, u32[]{:S(2)}, u32[]{:S(2)}) %collective-permute-start.23) | collective-permute-done | bytes 524320 | tf_op jit(solution)/shard_map/ppermute | solution.py:54
  385.6 4.3 copy.342
  389.9 4.8 copy.343
  397.7 8.1 collective-permute-done.12
  415.5 7.8 reshape.558
  423.3 11.2 copy.390
  434.5 6.5 copy.373
  445.0 6.4 copy.372
  451.4 15.5 %collective-permute-done.17 = bf16[3,1024,512]{2,1,0:T(8,128)(2,1)} collective-permute-done((bf16[3,1024,512]{2,1,0:T(8,128)(2,1)}, bf16[3,1024,512]{2,1,0:T(8,128)(2,1)}, u32[]{:S(2)}, u32[]{:S(2)}) %collective-permute-start.17) | collective-permute-done | bytes 3145760 | tf_op jit(solution)/shard_map/ppermute | solution.py:65
  466.9 67.0 %collective-permute-done.16 = bf16[3,1024,512]{2,1,0:T(8,128)(2,1)} collective-permute-done((bf16[3,1024,512]{2,1,0:T(8,128)(2,1)}, bf16[3,1024,512]{2,1,0:T(8,128)(2,1)}, u32[]{:S(2)}, u32[]{:S(2)}) %collective-permute-start.16) | collective-permute-done | bytes 3145760 | tf_op jit(solution)/shard_map/ppermute | solution.py:65
  533.8 14.6 %maximum_maximum_fusion = bf16[3,2048,1024]{2,1,0:T(8,128)(2,1)S(1)} fusion(bf16[3,1024,512]{2,1,0:T(8,128)(2,1)} %collective-permute-done.17, bf16[3,1024,512]{2,1,0:T(8,128)(2,1)} %collective-permute-done.16, bf16[3,1024,512]{2,1,0:T(8,128)(2,1)} %collective-permute-done.15, bf16[3,1024,512]{2,1,0:T(8,128)(2,1)} %bitcast.502), kind=kLoop, calls=%fused_computation.2 | loop fusion | flops 50331648 | bytes 25165824 | tf_op jit(solution)/shard_map/concatenate | solution.py:90
  548.5 6.2 fusion.23
  555.5 6.1 fusion.22
  561.6 5.3 copy.350
  566.9 14.0 %fusion.12 = (bf16[1024,1024]{1,0:T(8,128)(2,1)}, bf16[1024,1024]{1,0:T(8,128)(2,1)}, bf16[1024,1024]{1,0:T(8,128)(2,1)}, f32[1024,1024]{0,1:T(8,128)}) fusion(f32[1024,1024]{0,1:T(8,128)} %fusion.23, f32[1024,1024]{0,1:T(8,128)} %fusion.22, bf16[1024,2048]{1,0:T(8,128)(2,1)} %bitcast.482, bf16[3,2048,1024]{2,1,0:T(8,128)(2,1)} %copy-done.14), kind=kOutput, calls=%fused_computation.43 | convolution fusion | flops 4311744512 | bytes 27262976 | tf_op jit(solution)/shard_map/dot_general | solution.py:35
  580.9 5.4 copy.346
  586.3 5.3 copy.345
  591.7 9.3 convolution_convert_fusion.1
  601.0 10.3 fusion.20
  611.3 11.6 add_convert_fusion.1
  628.7 4.6 convolution_bitcast_fusion.1
  633.3 5.0 convolution_bitcast_fusion.2
  649.8 10.0 collective-permute-done.29
  659.7 22.3 %collective-permute-done.28 = bf16[128,2048]{1,0:T(8,128)(2,1)} collective-permute-done((bf16[128,2048]{1,0:T(8,128)(2,1)}, bf16[128,2048]{1,0:T(8,128)(2,1)}, u32[]{:S(2)}, u32[]{:S(2)}) %collective-permute-start.28) | collective-permute-done | bytes 524320 | tf_op jit(solution)/shard_map/ppermute | solution.py:54
  683.9 9.5 collective-permute-done.21
  693.4 32.7 %collective-permute-done.20 = bf16[128,2048]{1,0:T(8,128)(2,1)S(1)} collective-permute-done((bf16[128,2048]{1,0:T(8,128)(2,1)S(1)}, bf16[128,2048]{1,0:T(8,128)(2,1)S(1)}, u32[]{:S(2)}, u32[]{:S(2)}) %collective-permute-start.20) | collective-permute-done | bytes 524320 | tf_op jit(solution)/shard_map/ppermute | solution.py:54
  726.9 11.0 collective-permute-start.32
  739.4 7.1 convolution_bitcast_fusion
  750.4 33.8 %collective-permute-done.31 = bf16[128,2048]{1,0:T(8,128)(2,1)S(1)} collective-permute-done((bf16[128,2048]{1,0:T(8,128)(2,1)S(1)}, bf16[128,2048]{1,0:T(8,128)(2,1)S(1)}, u32[]{:S(2)}, u32[]{:S(2)}) %collective-permute-start.31) | collective-permute-done | bytes 524320 | tf_op jit(solution)/shard_map/ppermute | solution.py:54
  785.8 6.1 fusion.111
  799.4 12.5 %pad_maximum_fusion = f32[3,2,1024,2,512]{4,2,3,1,0:T(8,128)} fusion(f32[1,2,1024,2,512]{4,2,3,1,0:T(8,128)} %convolution_bitcast_fusion, f32[1,2,1024,2,512]{4,2,3,1,0:T(8,128)S(1)} %convolution_bitcast_fusion.1, f32[1,2,1024,2,512]{4,2,3,1,0:T(8,128)S(1)} %convolution_bitcast_fusion.2), kind=kLoop, calls=%fused_computation.1 | loop fusion | flops 12582912 | bytes 50331648 | tf_op jit(solution)/shard_map/stack | solution.py:213
  820.5 4.6 multiply_reduce_fusion.1
  825.1 4.8 multiply_convert_fusion
  845.0 23.0 %collective-permute-done.43 = bf16[3,1024,512]{2,1,0:T(8,128)(2,1)} collective-permute-done((bf16[3,1024,512]{2,1,0:T(8,128)(2,1)}, bf16[3,1024,512]{2,1,0:T(8,128)(2,1)}, u32[]{:S(2)}, u32[]{:S(2)}) %collective-permute-start.43) | collective-permute-done | bytes 3145760 | tf_op jit(solution)/shard_map/ppermute | solution.py:65
  868.1 78.2 %collective-permute-done.42 = bf16[3,1024,512]{2,1,0:T(8,128)(2,1)} collective-permute-done((bf16[3,1024,512]{2,1,0:T(8,128)(2,1)}, bf16[3,1024,512]{2,1,0:T(8,128)(2,1)}, u32[]{:S(2)}, u32[]{:S(2)}) %collective-permute-start.42) | collective-permute-done | bytes 3145760 | tf_op jit(solution)/shard_map/ppermute | solution.py:65
  946.3 7.2 fusion.5
  953.5 4.7 copy.377
  958.2 4.9 all-to-all-start.3
  963.1 6.6 copy.367
  994.9 52.5 %collective-permute-done.37 = bf16[128,2048]{1,0:T(8,128)(2,1)S(1)} collective-permute-done((bf16[128,2048]{1,0:T(8,128)(2,1)S(1)}, bf16[128,2048]{1,0:T(8,128)(2,1)S(1)}, u32[]{:S(2)}, u32[]{:S(2)}) %collective-permute-start.37) | collective-permute-done | bytes 524320 | tf_op jit(solution)/shard_map/ppermute | solution.py:54
  1048.9 42.4 %collective-permute-done.36 = bf16[128,2048]{1,0:T(8,128)(2,1)S(1)} collective-permute-done((bf16[128,2048]{1,0:T(8,128)(2,1)S(1)}, bf16[128,2048]{1,0:T(8,128)(2,1)S(1)}, u32[]{:S(2)}, u32[]{:S(2)}) %collective-permute-start.36) | collective-permute-done | bytes 524320 | tf_op jit(solution)/shard_map/ppermute | solution.py:54
  1100.9 20.4 %all-to-all-start.2 = ((bf16[4,1024,128]{2,0,1:T(4,128)(2,1)}), bf16[4,1024,128]{2,0,1:T(4,128)(2,1)S(1)}, u32[]{:S(2)}, u32[]{:S(2)}) async-start(bf16[4,1024,128]{2,0,1:T(4,128)(2,1)} %copy.371), calls=%async_computation.2 | async-start | bytes 2097152 | tf_op jit(solution)/shard_map/all_to_all | solution.py:100
  1129.7 4.7 copy.380
  1134.4 6.2 slice.219
  1140.6 4.3 copy.381
  1144.9 7.1 multiply_reduce_fusion
  1158.8 40.1 %psum.7 = f32[]{:T(128)} all-reduce(f32[]{:T(128)S(6)} %add.425), channel_id=1, replica_groups=mesh['fsdp'=2,'ctx'=4,'tp'=4] {'fsdp','ctx','tp'}, use_global_device_ids=true, to_apply=%region_15.16 | all-reduce | flops 1 | bytes 8 | tf_op jit(solution)/shard_map/psum | solution.py:248
  1206.5 5.0 fusion.120
  1211.6 6.6 fusion.114
  1220.0 6.4 fusion.116
  (350 shorter events, 202.8 us)
Async XLA Ops:
  8.6 319.1 %copy-start.9 = (bf16[1,128,1024]{2,1,0:T(8,128)(2,1)}, bf16[1,128,1024]{2,1,0:T(8,128)(2,1)S(1)}, u32[]{:S(2)}) copy-start(bf16[1,128,1024]{2,1,0:T(8,128)(2,1)S(1)} %get-tuple-element.92) | copy-start | bytes 786436
  8.7 319.1 %copy-start.11 = (bf16[1,128,1024]{2,1,0:T(8,128)(2,1)}, bf16[1,128,1024]{2,1,0:T(8,128)(2,1)S(1)}, u32[]{:S(2)}) copy-start(bf16[1,128,1024]{2,1,0:T(8,128)(2,1)S(1)} %get-tuple-element.93) | copy-start | bytes 786436
  10.2 17.7 %collective-permute-start.2 = (bf16[128,2048]{1,0:T(8,128)(2,1)}, bf16[128,2048]{1,0:T(8,128)(2,1)}, u32[]{:S(2)}, u32[]{:S(2)}) collective-permute-start(bf16[128,2048]{1,0:T(8,128)(2,1)} %fusion.49), channel_id=1, source_target_pairs={{0,12},{4,0},{8,4},{12,8},{1,13},{5,1},{9,5},{13,9},{2,14},{6,2},{... | collective-permute-start | bytes 1572872 | tf_op jit(solution)/shard_map/ppermute | solution.py:54
  15.3 57.5 %collective-permute-start.1 = (bf16[128,2048]{1,0:T(8,128)(2,1)}, bf16[128,2048]{1,0:T(8,128)(2,1)}, u32[]{:S(2)}, u32[]{:S(2)}) collective-permute-start(bf16[128,2048]{1,0:T(8,128)(2,1)} %fusion.49), channel_id=1, source_target_pairs={{0,8},{4,12},{8,0},{12,4},{1,9},{5,13},{9,1},{13,5},{2,10},{6,14},... | collective-permute-start | bytes 1572872 | tf_op jit(solution)/shard_map/ppermute | solution.py:54
  15.3 57.5 %collective-permute-start = (bf16[128,2048]{1,0:T(8,128)(2,1)}, bf16[128,2048]{1,0:T(8,128)(2,1)}, u32[]{:S(2)}, u32[]{:S(2)}) collective-permute-start(bf16[128,2048]{1,0:T(8,128)(2,1)} %fusion.49), channel_id=1, source_target_pairs={{0,4},{4,8},{8,12},{12,0},{1,5},{5,9},{9,13},{13,1},{2,6},{6,10},{... | collective-permute-start | bytes 1572872 | tf_op jit(solution)/shard_map/ppermute | solution.py:54
  19.0 63.7 %all-to-all-start = ((bf16[4,256,512]{1,0,2:T(4,128)(2,1)}), bf16[4,256,512]{1,0,2:T(4,128)(2,1)S(1)}, u32[]{:S(2)}, u32[]{:S(2)}) async-start(bf16[4,256,512]{1,0,2:T(4,128)(2,1)} %copy.331), calls=%async_computation | async-start | bytes 2097152 | tf_op jit(solution)/shard_map/all_to_all | solution.py:83
  76.5 14.1 %collective-permute-start.3 = (bf16[4,128,2048]{2,1,0:T(8,128)(2,1)}, bf16[4,128,2048]{2,1,0:T(8,128)(2,1)}, u32[]{:S(2)}, u32[]{:S(2)}) collective-permute-start(bf16[4,128,2048]{2,1,0:T(8,128)(2,1)} %get-tuple-element.91), channel_id=1, source_target_pairs={{0,1},{1,0},{2,3},{3,2},{4,5},{5,4},{6,7},{7,6},{8,9},{9,8},{10,11... | collective-permute-start | bytes 6291464 | tf_op jit(solution)/shard_map/ppermute | solution.py:57
  84.3 27.1 %collective-permute-start.6 = (bf16[4,1024,128]{1,2,0:T(8,128)(2,1)S(1)}, bf16[4,1024,128]{1,2,0:T(8,128)(2,1)S(1)}, u32[]{:S(2)}, u32[]{:S(2)}) collective-permute-start(bf16[4,1024,128]{1,2,0:T(8,128)(2,1)S(1)} %all_to_all.43), channel_id=1, source_target_pairs={{0,18},{1,19},{2,16},{3,17},{16,2},{17,3},{18,0},{19,1},{4,22},{5,... | collective-permute-start | bytes 3145736 | tf_op jit(solution)/shard_map/ppermute | solution.py:65
  86.8 44.9 %collective-permute-start.5 = (bf16[4,1024,128]{1,2,0:T(8,128)(2,1)S(1)}, bf16[4,1024,128]{1,2,0:T(8,128)(2,1)S(1)}, u32[]{:S(2)}, u32[]{:S(2)}) collective-permute-start(bf16[4,1024,128]{1,2,0:T(8,128)(2,1)S(1)} %all_to_all.43), channel_id=1, source_target_pairs={{0,2},{1,3},{2,0},{3,1},{16,18},{17,19},{18,16},{19,17},{4,6},{5,7... | collective-permute-start | bytes 3145736 | tf_op jit(solution)/shard_map/ppermute | solution.py:65
  87.3 44.5 %collective-permute-start.4 = (bf16[4,1024,128]{1,2,0:T(8,128)(2,1)S(1)}, bf16[4,1024,128]{1,2,0:T(8,128)(2,1)S(1)}, u32[]{:S(2)}, u32[]{:S(2)}) collective-permute-start(bf16[4,1024,128]{1,2,0:T(8,128)(2,1)S(1)} %all_to_all.43), channel_id=1, source_target_pairs={{0,16},{1,17},{2,18},{3,19},{16,0},{17,1},{18,2},{19,3},{4,20},{5,... | collective-permute-start | bytes 3145736 | tf_op jit(solution)/shard_map/ppermute | solution.py:65
  89.7 47.2 %copy-start.35 = (f32[1024,64]{0,1:T(8,128)}, f32[1024,64]{0,1:T(8,128)S(1)}, u32[]{:S(2)}) copy-start(f32[1024,64]{0,1:T(8,128)S(1)} %get-tuple-element.115) | copy-start | bytes 786436
  93.8 41.8 %copy-start.5 = (bf16[4,2,128,2048]{3,2,1,0:T(8,128)(2,1)}, bf16[4,2,128,2048]{3,2,1,0:T(8,128)(2,1)S(1)}, u32[]{:S(2)}) copy-start(bf16[4,2,128,2048]{3,2,1,0:T(8,128)(2,1)S(1)} %copy.330) | copy-start | bytes 12582916
  153.9 23.1 %collective-permute-start.7 = (bf16[4,128,2048]{2,1,0:T(8,128)(2,1)}, bf16[4,128,2048]{2,1,0:T(8,128)(2,1)}, u32[]{:S(2)}, u32[]{:S(2)}) collective-permute-start(bf16[4,128,2048]{2,1,0:T(8,128)(2,1)} %slice_bitcast_fusion.20), channel_id=1, source_target_pairs={{0,1},{1,0},{2,3},{3,2},{4,5},{5,4},{6,7},{7,6},{8,9},{9,8},{10,11... | collective-permute-start | bytes 6291464 | tf_op jit(solution)/shard_map/ppermute | solution.py:57
  171.8 213.8 %all-to-all-start.1 = ((bf16[3,256,2048]{1,0,2:T(4,128)(2,1)}), bf16[3,256,2048]{1,0,2:T(4,128)(2,1)}, u32[]{:S(2)}, u32[]{:S(2)}) async-start(bf16[3,256,2048]{1,0,2:T(4,128)(2,1)} %pad_maximum_fusion.4), calls=%async_computation.1 | async-start | bytes 8388608 | tf_op jit(solution)/shard_map/all_to_all | solution.py:83
  177.0 944.3 %all-gather.3.cloned.1.call-start = ((), (), s32[]{:S(2)}) async-start(), calls=%async_computation.4 | async-start | bytes 2621440 | tf_op jit(solution)/shard_map/all_gather | solution.py:212
  180.3 81.0 %collective-permute-start.10 = (bf16[128,2048]{1,0:T(8,128)(2,1)S(1)}, bf16[128,2048]{1,0:T(8,128)(2,1)S(1)}, u32[]{:S(2)}, u32[]{:S(2)}) collective-permute-start(bf16[128,2048]{1,0:T(8,128)(2,1)S(1)} %get-tuple-element.88), channel_id=1, source_target_pairs={{0,4},{4,8},{8,12},{12,0},{1,5},{5,9},{9,13},{13,1},{2,6},{6,10},{... | collective-permute-start | bytes 1572872 | tf_op jit(solution)/shard_map/ppermute | solution.py:54
  182.4 145.3 %collective-permute-start.9 = (bf16[128,2048]{1,0:T(8,128)(2,1)S(1)}, bf16[128,2048]{1,0:T(8,128)(2,1)S(1)}, u32[]{:S(2)}, u32[]{:S(2)}) collective-permute-start(bf16[128,2048]{1,0:T(8,128)(2,1)S(1)} %get-tuple-element.89), channel_id=1, source_target_pairs={{0,8},{4,12},{8,0},{12,4},{1,9},{5,13},{9,1},{13,5},{2,10},{6,14},... | collective-permute-start | bytes 1572872 | tf_op jit(solution)/shard_map/ppermute | solution.py:54
  184.8 143.0 %collective-permute-start.8 = (bf16[128,2048]{1,0:T(8,128)(2,1)S(1)}, bf16[128,2048]{1,0:T(8,128)(2,1)S(1)}, u32[]{:S(2)}, u32[]{:S(2)}) collective-permute-start(bf16[128,2048]{1,0:T(8,128)(2,1)S(1)} %get-tuple-element.87), channel_id=1, source_target_pairs={{0,12},{4,0},{8,4},{12,8},{1,13},{5,1},{9,5},{13,9},{2,14},{6,2},{... | collective-permute-start | bytes 1572872 | tf_op jit(solution)/shard_map/ppermute | solution.py:54
  187.5 142.0 %copy-start.37 = (bf16[128,1024]{1,0:T(8,128)(2,1)}, bf16[128,1024]{1,0:T(8,128)(2,1)S(1)}, u32[]{:S(2)}) copy-start(bf16[128,1024]{1,0:T(8,128)(2,1)S(1)} %get-tuple-element.81) | copy-start | bytes 786436
  187.6 155.2 %collective-permute-start.24 = (bf16[128,2048]{1,0:T(8,128)(2,1)S(1)}, bf16[128,2048]{1,0:T(8,128)(2,1)S(1)}, u32[]{:S(2)}, u32[]{:S(2)}) collective-permute-start(bf16[128,2048]{1,0:T(8,128)(2,1)S(1)} %get-tuple-element.108), channel_id=1, source_target_pairs={{0,12},{4,0},{8,4},{12,8},{1,13},{5,1},{9,5},{13,9},{2,14},{6,2},{... | collective-permute-start | bytes 1572872 | tf_op jit(solution)/shard_map/ppermute | solution.py:54
  188.2 195.7 %collective-permute-start.23 = (bf16[128,2048]{1,0:T(8,128)(2,1)S(1)}, bf16[128,2048]{1,0:T(8,128)(2,1)S(1)}, u32[]{:S(2)}, u32[]{:S(2)}) collective-permute-start(bf16[128,2048]{1,0:T(8,128)(2,1)S(1)} %get-tuple-element.108), channel_id=1, source_target_pairs={{0,8},{4,12},{8,0},{12,4},{1,9},{5,13},{9,1},{13,5},{2,10},{6,14},... | collective-permute-start | bytes 1572872 | tf_op jit(solution)/shard_map/ppermute | solution.py:54
  261.3 122.6 %collective-permute-start.22 = (bf16[128,2048]{1,0:T(8,128)(2,1)S(1)}, bf16[128,2048]{1,0:T(8,128)(2,1)S(1)}, u32[]{:S(2)}, u32[]{:S(2)}) collective-permute-start(bf16[128,2048]{1,0:T(8,128)(2,1)S(1)} %get-tuple-element.108), channel_id=1, source_target_pairs={{0,4},{4,8},{8,12},{12,0},{1,5},{5,9},{9,13},{13,1},{2,6},{6,10},{... | collective-permute-start | bytes 1572872 | tf_op jit(solution)/shard_map/ppermute | solution.py:54
  329.5 66.8 %collective-permute-start.13 = (bf16[128,2048]{1,0:T(8,128)(2,1)}, bf16[128,2048]{1,0:T(8,128)(2,1)}, u32[]{:S(2)}, u32[]{:S(2)}) collective-permute-start(bf16[128,2048]{1,0:T(8,128)(2,1)} %fusion.76), channel_id=1, source_target_pairs={{0,12},{4,0},{8,4},{12,8},{1,13},{5,1},{9,5},{13,9},{2,14},{6,2},{... | collective-permute-start | bytes 1572872 | tf_op jit(solution)/shard_map/ppermute | solution.py:54
  342.3 63.5 %collective-permute-start.12 = (bf16[128,2048]{1,0:T(8,128)(2,1)}, bf16[128,2048]{1,0:T(8,128)(2,1)}, u32[]{:S(2)}, u32[]{:S(2)}) collective-permute-start(bf16[128,2048]{1,0:T(8,128)(2,1)} %fusion.76), channel_id=1, source_target_pairs={{0,8},{4,12},{8,0},{12,4},{1,9},{5,13},{9,1},{13,5},{2,10},{6,14},... | collective-permute-start | bytes 1572872 | tf_op jit(solution)/shard_map/ppermute | solution.py:54
  342.8 64.7 %collective-permute-start.11 = (bf16[128,2048]{1,0:T(8,128)(2,1)}, bf16[128,2048]{1,0:T(8,128)(2,1)}, u32[]{:S(2)}, u32[]{:S(2)}) collective-permute-start(bf16[128,2048]{1,0:T(8,128)(2,1)} %fusion.76), channel_id=1, source_target_pairs={{0,4},{4,8},{8,12},{12,0},{1,5},{5,9},{9,13},{13,1},{2,6},{6,10},{... | collective-permute-start | bytes 1572872 | tf_op jit(solution)/shard_map/ppermute | solution.py:54
  385.6 25.6 %collective-permute-start.25 = (bf16[4,128,2048]{2,1,0:T(8,128)(2,1)}, bf16[4,128,2048]{2,1,0:T(8,128)(2,1)}, u32[]{:S(2)}, u32[]{:S(2)}) collective-permute-start(bf16[4,128,2048]{2,1,0:T(8,128)(2,1)} %get-tuple-element.79), channel_id=1, source_target_pairs={{0,1},{1,0},{2,3},{3,2},{4,5},{5,4},{6,7},{7,6},{8,9},{9,8},{10,11... | collective-permute-start | bytes 6291464 | tf_op jit(solution)/shard_map/ppermute | solution.py:57
  394.7 72.2 %collective-permute-start.17 = (bf16[3,1024,512]{2,1,0:T(8,128)(2,1)}, bf16[3,1024,512]{2,1,0:T(8,128)(2,1)}, u32[]{:S(2)}, u32[]{:S(2)}) collective-permute-start(bf16[3,1024,512]{2,1,0:T(8,128)(2,1)} %bitcast.499), channel_id=1, source_target_pairs={{0,18},{1,19},{2,16},{3,17},{16,2},{17,3},{18,0},{19,1},{4,22},{5,... | collective-permute-start | bytes 9437192 | tf_op jit(solution)/shard_map/ppermute | solution.py:65
  396.3 137.5 %collective-permute-start.16 = (bf16[3,1024,512]{2,1,0:T(8,128)(2,1)}, bf16[3,1024,512]{2,1,0:T(8,128)(2,1)}, u32[]{:S(2)}, u32[]{:S(2)}) collective-permute-start(bf16[3,1024,512]{2,1,0:T(8,128)(2,1)} %bitcast.500), channel_id=1, source_target_pairs={{0,2},{1,3},{2,0},{3,1},{16,18},{17,19},{18,16},{19,17},{4,6},{5,7... | collective-permute-start | bytes 9437192 | tf_op jit(solution)/shard_map/ppermute | solution.py:65
  405.8 128.1 %collective-permute-start.15 = (bf16[3,1024,512]{2,1,0:T(8,128)(2,1)}, bf16[3,1024,512]{2,1,0:T(8,128)(2,1)}, u32[]{:S(2)}, u32[]{:S(2)}) collective-permute-start(bf16[3,1024,512]{2,1,0:T(8,128)(2,1)} %bitcast.501), channel_id=1, source_target_pairs={{0,16},{1,17},{2,18},{3,19},{16,0},{17,1},{18,2},{19,3},{4,20},{5,... | collective-permute-start | bytes 9437192 | tf_op jit(solution)/shard_map/ppermute | solution.py:65
  411.2 29.8 %collective-permute-start.14 = (bf16[4,128,2048]{2,1,0:T(8,128)(2,1)}, bf16[4,128,2048]{2,1,0:T(8,128)(2,1)}, u32[]{:S(2)}, u32[]{:S(2)}) collective-permute-start(bf16[4,128,2048]{2,1,0:T(8,128)(2,1)} %get-tuple-element.86), channel_id=1, source_target_pairs={{0,1},{1,0},{2,3},{3,2},{4,5},{5,4},{6,7},{7,6},{8,9},{9,8},{10,11... | collective-permute-start | bytes 6291464 | tf_op jit(solution)/shard_map/ppermute | solution.py:57
  451.4 97.0 %copy-start.7 = (bf16[4,2,128,2048]{3,2,1,0:T(8,128)(2,1)S(1)}, bf16[4,2,128,2048]{3,2,1,0:T(8,128)(2,1)}, u32[]{:S(2)}) copy-start(bf16[4,2,128,2048]{3,2,1,0:T(8,128)(2,1)} %copy.349) | copy-start | bytes 12582916
  624.5 13.8 %collective-permute-start.26 = (bf16[4,128,2048]{2,1,0:T(8,128)(2,1)}, bf16[4,128,2048]{2,1,0:T(8,128)(2,1)}, u32[]{:S(2)}, u32[]{:S(2)}) collective-permute-start(bf16[4,128,2048]{2,1,0:T(8,128)(2,1)} %slice_bitcast_fusion.16), channel_id=1, source_target_pairs={{0,1},{1,0},{2,3},{3,2},{4,5},{5,4},{6,7},{7,6},{8,9},{9,8},{10,11... | collective-permute-start | bytes 6291464 | tf_op jit(solution)/shard_map/ppermute | solution.py:57
  627.0 19.5 %collective-permute-start.18 = (bf16[4,128,2048]{2,1,0:T(8,128)(2,1)}, bf16[4,128,2048]{2,1,0:T(8,128)(2,1)S(1)}, u32[]{:S(2)}, u32[]{:S(2)}) collective-permute-start(bf16[4,128,2048]{2,1,0:T(8,128)(2,1)} %slice_bitcast_fusion.18), channel_id=1, source_target_pairs={{0,1},{1,0},{2,3},{3,2},{4,5},{5,4},{6,7},{7,6},{8,9},{9,8},{10,11... | collective-permute-start | bytes 6291464 | tf_op jit(solution)/shard_map/ppermute | solution.py:57
  642.7 17.0 %collective-permute-start.29 = (bf16[128,2048]{1,0:T(8,128)(2,1)}, bf16[128,2048]{1,0:T(8,128)(2,1)}, u32[]{:S(2)}, u32[]{:S(2)}) collective-permute-start(bf16[128,2048]{1,0:T(8,128)(2,1)} %get-tuple-element.76), channel_id=1, source_target_pairs={{0,4},{4,8},{8,12},{12,0},{1,5},{5,9},{9,13},{13,1},{2,6},{6,10},{... | collective-permute-start | bytes 1572872 | tf_op jit(solution)/shard_map/ppermute | solution.py:54
  642.7 39.4 %collective-permute-start.28 = (bf16[128,2048]{1,0:T(8,128)(2,1)}, bf16[128,2048]{1,0:T(8,128)(2,1)}, u32[]{:S(2)}, u32[]{:S(2)}) collective-permute-start(bf16[128,2048]{1,0:T(8,128)(2,1)} %get-tuple-element.77), channel_id=1, source_target_pairs={{0,8},{4,12},{8,0},{12,4},{1,9},{5,13},{9,1},{13,5},{2,10},{6,14},... | collective-permute-start | bytes 1572872 | tf_op jit(solution)/shard_map/ppermute | solution.py:54
  643.3 38.7 %collective-permute-start.27 = (bf16[128,2048]{1,0:T(8,128)(2,1)}, bf16[128,2048]{1,0:T(8,128)(2,1)}, u32[]{:S(2)}, u32[]{:S(2)}) collective-permute-start(bf16[128,2048]{1,0:T(8,128)(2,1)} %get-tuple-element.75), channel_id=1, source_target_pairs={{0,12},{4,0},{8,4},{12,8},{1,13},{5,1},{9,5},{13,9},{2,14},{6,2},{... | collective-permute-start | bytes 1572872 | tf_op jit(solution)/shard_map/ppermute | solution.py:54
  647.5 78.6 %copy-start.38 = (bf16[128,1024]{1,0:T(8,128)(2,1)S(1)}, bf16[128,1024]{1,0:T(8,128)(2,1)}, u32[]{:S(2)}) copy-start(bf16[128,1024]{1,0:T(8,128)(2,1)} %copy-done.37) | copy-start | bytes 786436
  647.6 45.8 %collective-permute-start.21 = (bf16[128,2048]{1,0:T(8,128)(2,1)S(1)}, bf16[128,2048]{1,0:T(8,128)(2,1)S(1)}, u32[]{:S(2)}, u32[]{:S(2)}) collective-permute-start(bf16[128,2048]{1,0:T(8,128)(2,1)S(1)} %get-tuple-element.83), channel_id=1, source_target_pairs={{0,4},{4,8},{8,12},{12,0},{1,5},{5,9},{9,13},{13,1},{2,6},{6,10},{... | collective-permute-start | bytes 1572872 | tf_op jit(solution)/shard_map/ppermute | solution.py:54
  648.2 77.9 %collective-permute-start.20 = (bf16[128,2048]{1,0:T(8,128)(2,1)S(1)}, bf16[128,2048]{1,0:T(8,128)(2,1)S(1)}, u32[]{:S(2)}, u32[]{:S(2)}) collective-permute-start(bf16[128,2048]{1,0:T(8,128)(2,1)S(1)} %get-tuple-element.84), channel_id=1, source_target_pairs={{0,8},{4,12},{8,0},{12,4},{1,9},{5,13},{9,1},{13,5},{2,10},{6,14},... | collective-permute-start | bytes 1572872 | tf_op jit(solution)/shard_map/ppermute | solution.py:54
  659.7 66.4 %collective-permute-start.19 = (bf16[128,2048]{1,0:T(8,128)(2,1)S(1)}, bf16[128,2048]{1,0:T(8,128)(2,1)S(1)}, u32[]{:S(2)}, u32[]{:S(2)}) collective-permute-start(bf16[128,2048]{1,0:T(8,128)(2,1)S(1)} %get-tuple-element.82), channel_id=1, source_target_pairs={{0,12},{4,0},{8,4},{12,8},{1,13},{5,1},{9,5},{13,9},{2,14},{6,2},{... | collective-permute-start | bytes 1572872 | tf_op jit(solution)/shard_map/ppermute | solution.py:54
  683.9 55.5 %copy-start.28 = (bf16[2048,1024]{1,0:T(8,128)(2,1)S(1)}, bf16[2048,1024]{1,0:T(8,128)(2,1)}, u32[]{:S(2)}) copy-start(bf16[2048,1024]{1,0:T(8,128)(2,1)} %copy.373) | copy-start | bytes 12582916
  683.9 55.5 %copy-start.70 = (bf16[1024,1024]{1,0:T(8,128)(2,1)S(1)}, bf16[1024,1024]{1,0:T(8,128)(2,1)}, u32[]{:S(2)}) copy-start(bf16[1024,1024]{1,0:T(8,128)(2,1)} %get-tuple-element.55) | copy-start | bytes 6291460
  726.9 23.4 %collective-permute-start.32 = (bf16[128,2048]{1,0:T(8,128)(2,1)S(1)}, bf16[128,2048]{1,0:T(8,128)(2,1)S(1)}, u32[]{:S(2)}, u32[]{:S(2)}) collective-permute-start(bf16[128,2048]{1,0:T(8,128)(2,1)S(1)} %get-tuple-element.45), channel_id=1, source_target_pairs={{0,12},{4,0},{8,4},{12,8},{1,13},{5,1},{9,5},{13,9},{2,14},{6,2},{... | collective-permute-start | bytes 1572872 | tf_op jit(solution)/shard_map/ppermute | solution.py:54
  737.9 46.2 %collective-permute-start.31 = (bf16[128,2048]{1,0:T(8,128)(2,1)S(1)}, bf16[128,2048]{1,0:T(8,128)(2,1)S(1)}, u32[]{:S(2)}, u32[]{:S(2)}) collective-permute-start(bf16[128,2048]{1,0:T(8,128)(2,1)S(1)} %get-tuple-element.45), channel_id=1, source_target_pairs={{0,8},{4,12},{8,0},{12,4},{1,9},{5,13},{9,1},{13,5},{2,10},{6,14},... | collective-permute-start | bytes 1572872 | tf_op jit(solution)/shard_map/ppermute | solution.py:54
  739.4 44.8 %collective-permute-start.30 = (bf16[128,2048]{1,0:T(8,128)(2,1)S(1)}, bf16[128,2048]{1,0:T(8,128)(2,1)S(1)}, u32[]{:S(2)}, u32[]{:S(2)}) collective-permute-start(bf16[128,2048]{1,0:T(8,128)(2,1)S(1)} %get-tuple-element.45), channel_id=1, source_target_pairs={{0,4},{4,8},{8,12},{12,0},{1,5},{5,9},{9,13},{13,1},{2,6},{6,10},{... | collective-permute-start | bytes 1572872 | tf_op jit(solution)/shard_map/ppermute | solution.py:54
  785.8 27.0 %collective-permute-start.33 = (bf16[4,128,2048]{2,1,0:T(8,128)(2,1)}, bf16[4,128,2048]{2,1,0:T(8,128)(2,1)}, u32[]{:S(2)}, u32[]{:S(2)}) collective-permute-start(bf16[4,128,2048]{2,1,0:T(8,128)(2,1)} %get-tuple-element.74), channel_id=1, source_target_pairs={{0,1},{1,0},{2,3},{3,2},{4,5},{5,4},{6,7},{7,6},{8,9},{9,8},{10,11... | collective-permute-start | bytes 6291464 | tf_op jit(solution)/shard_map/ppermute | solution.py:57
  795.9 72.2 %collective-permute-start.43 = (bf16[3,1024,512]{2,1,0:T(8,128)(2,1)}, bf16[3,1024,512]{2,1,0:T(8,128)(2,1)}, u32[]{:S(2)}, u32[]{:S(2)}) collective-permute-start(bf16[3,1024,512]{2,1,0:T(8,128)(2,1)} %get-tuple-element.51), channel_id=1, source_target_pairs={{0,18},{1,19},{2,16},{3,17},{16,2},{17,3},{18,0},{19,1},{4,22},{5,... | collective-permute-start | bytes 9437192 | tf_op jit(solution)/shard_map/ppermute | solution.py:65
  797.6 148.7 %collective-permute-start.42 = (bf16[3,1024,512]{2,1,0:T(8,128)(2,1)}, bf16[3,1024,512]{2,1,0:T(8,128)(2,1)}, u32[]{:S(2)}, u32[]{:S(2)}) collective-permute-start(bf16[3,1024,512]{2,1,0:T(8,128)(2,1)} %get-tuple-element.52), channel_id=1, source_target_pairs={{0,2},{1,3},{2,0},{3,1},{16,18},{17,19},{18,16},{19,17},{4,6},{5,7... | collective-permute-start | bytes 9437192 | tf_op jit(solution)/shard_map/ppermute | solution.py:65
  798.9 147.4 %collective-permute-start.41 = (bf16[3,1024,512]{2,1,0:T(8,128)(2,1)}, bf16[3,1024,512]{2,1,0:T(8,128)(2,1)}, u32[]{:S(2)}, u32[]{:S(2)}) collective-permute-start(bf16[3,1024,512]{2,1,0:T(8,128)(2,1)} %get-tuple-element.50), channel_id=1, source_target_pairs={{0,16},{1,17},{2,18},{3,19},{16,0},{17,1},{18,2},{19,3},{4,20},{5,... | collective-permute-start | bytes 9437192 | tf_op jit(solution)/shard_map/ppermute | solution.py:65
  845.0 135.0 %collective-permute-start.34 = (bf16[4,128,2048]{2,1,0:T(8,128)(2,1)}, bf16[4,128,2048]{2,1,0:T(8,128)(2,1)}, u32[]{:S(2)}, u32[]{:S(2)}) collective-permute-start(bf16[4,128,2048]{2,1,0:T(8,128)(2,1)} %slice_bitcast_fusion.14), channel_id=1, source_target_pairs={{0,1},{1,0},{2,3},{3,2},{4,5},{5,4},{6,7},{7,6},{8,9},{9,8},{10,11... | collective-permute-start | bytes 6291464 | tf_op jit(solution)/shard_map/ppermute | solution.py:57
  958.2 142.7 %all-to-all-start.3 = ((bf16[3,1024,512]{2,0,1:T(4,128)(2,1)}), bf16[3,1024,512]{2,0,1:T(4,128)(2,1)}, u32[]{:S(2)}, u32[]{:S(2)}) async-start(bf16[3,1024,512]{2,0,1:T(4,128)(2,1)} %copy.377), calls=%async_computation.3 | async-start | bytes 8388608 | tf_op jit(solution)/shard_map/all_to_all | solution.py:100
  963.1 263.3 %all-gather.5.cloned.1.call-start = ((), (), s32[]{:S(2)}) async-start(), calls=%async_computation.5 | async-start | bytes 5242880 | tf_op jit(solution)/shard_map/all_gather | solution.py:242
  974.8 14.3 %copy-start.19 = (f32[1,2,1024,2,128]{4,2,3,1,0:T(8,128)}, f32[1,2,1024,2,128]{4,2,3,1,0:T(8,128)S(1)}, u32[]{:S(2)}) copy-start(f32[1,2,1024,2,128]{4,2,3,1,0:T(8,128)S(1)} %convolution_bitcast_fusion.6) | copy-start | bytes 6291460
  983.4 64.0 %collective-permute-start.37 = (bf16[128,2048]{1,0:T(8,128)(2,1)S(1)}, bf16[128,2048]{1,0:T(8,128)(2,1)S(1)}, u32[]{:S(2)}, u32[]{:S(2)}) collective-permute-start(bf16[128,2048]{1,0:T(8,128)(2,1)S(1)} %get-tuple-element.71), channel_id=1, source_target_pairs={{0,4},{4,8},{8,12},{12,0},{1,5},{5,9},{9,13},{13,1},{2,6},{6,10},{... | collective-permute-start | bytes 1572872 | tf_op jit(solution)/shard_map/ppermute | solution.py:54
  985.3 105.9 %collective-permute-start.36 = (bf16[128,2048]{1,0:T(8,128)(2,1)S(1)}, bf16[128,2048]{1,0:T(8,128)(2,1)S(1)}, u32[]{:S(2)}, u32[]{:S(2)}) collective-permute-start(bf16[128,2048]{1,0:T(8,128)(2,1)S(1)} %get-tuple-element.72), channel_id=1, source_target_pairs={{0,8},{4,12},{8,0},{12,4},{1,9},{5,13},{9,1},{13,5},{2,10},{6,14},... | collective-permute-start | bytes 1572872 | tf_op jit(solution)/shard_map/ppermute | solution.py:54
  987.7 103.6 %collective-permute-start.35 = (bf16[128,2048]{1,0:T(8,128)(2,1)S(1)}, bf16[128,2048]{1,0:T(8,128)(2,1)S(1)}, u32[]{:S(2)}, u32[]{:S(2)}) collective-permute-start(bf16[128,2048]{1,0:T(8,128)(2,1)S(1)} %get-tuple-element.70), channel_id=1, source_target_pairs={{0,12},{4,0},{8,4},{12,8},{1,13},{5,1},{9,5},{13,9},{2,14},{6,2},{... | collective-permute-start | bytes 1572872 | tf_op jit(solution)/shard_map/ppermute | solution.py:54
  990.1 101.2 %copy-start.10 = (bf16[1,128,1024]{2,1,0:T(8,128)(2,1)S(1)}, bf16[1,128,1024]{2,1,0:T(8,128)(2,1)}, u32[]{:S(2)}) copy-start(bf16[1,128,1024]{2,1,0:T(8,128)(2,1)} %copy-done.9) | copy-start | bytes 786436
  990.1 101.2 %copy-start.12 = (bf16[1,128,1024]{2,1,0:T(8,128)(2,1)S(1)}, bf16[1,128,1024]{2,1,0:T(8,128)(2,1)}, u32[]{:S(2)}) copy-start(bf16[1,128,1024]{2,1,0:T(8,128)(2,1)} %copy-done.11) | copy-start | bytes 786436
  990.2 101.1 %copy-start.63 = (f32[128]{0:T(128)S(1)}, f32[128]{0:T(128)}, u32[]{:S(2)}) copy-start(f32[128]{0:T(128)} %copy-done.62) | copy-start | bytes 1540
  990.2 101.1 %copy-start.67 = (f32[128]{0:T(128)S(1)}, f32[128]{0:T(128)}, u32[]{:S(2)}) copy-start(f32[128]{0:T(128)} %copy-done.66) | copy-start | bytes 1540
  991.9 104.8 %collective-permute-start.40 = (bf16[4,1024,128]{2,1,0:T(8,128)(2,1)}, bf16[4,1024,128]{2,1,0:T(8,128)(2,1)}, u32[]{:S(2)}, u32[]{:S(2)}) collective-permute-start(bf16[4,1024,128]{2,1,0:T(8,128)(2,1)} %get-tuple-element.65), channel_id=1, source_target_pairs={{0,18},{1,19},{2,16},{3,17},{16,2},{17,3},{18,0},{19,1},{4,22},{5,... | collective-permute-start | bytes 3145736 | tf_op jit(solution)/shard_map/ppermute | solution.py:65
  993.6 103.2 %collective-permute-start.39 = (bf16[4,1024,128]{2,1,0:T(8,128)(2,1)}, bf16[4,1024,128]{2,1,0:T(8,128)(2,1)}, u32[]{:S(2)}, u32[]{:S(2)}) collective-permute-start(bf16[4,1024,128]{2,1,0:T(8,128)(2,1)} %get-tuple-element.66), channel_id=1, source_target_pairs={{0,2},{1,3},{2,0},{3,1},{16,18},{17,19},{18,16},{19,17},{4,6},{5,7... | collective-permute-start | bytes 3145736 | tf_op jit(solution)/shard_map/ppermute | solution.py:65
  1047.4 49.4 %collective-permute-start.38 = (bf16[4,1024,128]{2,1,0:T(8,128)(2,1)}, bf16[4,1024,128]{2,1,0:T(8,128)(2,1)}, u32[]{:S(2)}, u32[]{:S(2)}) collective-permute-start(bf16[4,1024,128]{2,1,0:T(8,128)(2,1)} %get-tuple-element.64), channel_id=1, source_target_pairs={{0,16},{1,17},{2,18},{3,19},{16,0},{17,1},{18,2},{19,3},{4,20},{5,... | collective-permute-start | bytes 3145736 | tf_op jit(solution)/shard_map/ppermute | solution.py:65
  1100.9 51.1 %all-to-all-start.2 = ((bf16[4,1024,128]{2,0,1:T(4,128)(2,1)}), bf16[4,1024,128]{2,0,1:T(4,128)(2,1)S(1)}, u32[]{:S(2)}, u32[]{:S(2)}) async-start(bf16[4,1024,128]{2,0,1:T(4,128)(2,1)} %copy.371), calls=%async_computation.2 | async-start | bytes 2097152 | tf_op jit(solution)/shard_map/all_to_all | solution.py:100
  (65 other events, 353.0 us)
Sparse Core Ops, SparseCore 0:
  812.9 78.6 all-gather.2
  1093.7 43.1 all-gather.4
where the time goes:
time: 1250 us; the launch traced here: 1240 us
  waiting for transfers between devices  598 us (48%)
  starting transfers between devices  175 us (14%)
  local copies, waits for them, and re-layouts  154 us (12%)
  other arithmetic  139 us (11%)
  matrix products  114 us (9%)
  blocking collectives  40.1 us (3%)
  between operations  19.1 us (2%)
    ppermute x24, waiting for transfers between devices, by_ctx(): lax.ppermute(block, 'ctx', [(i, (i + shift) % n_c) for i in range(n_c)])  370 us
    ppermute x12, waiting for transfers between devices, by_pack(): return lax.ppermute(block, ('fsdp', 'tp'), pairs)  222 us
    ppermute x24, starting transfers between devices, by_ctx(): lax.ppermute(block, 'ctx', [(i, (i + shift) % n_c) for i in range(n_c)])  125 us
    dot_general x21, matrix products, dot(): lax.dot_general(left, right, (dims, ((), ())), preferred_element_type=F32)  95.9 us
    psum x1, blocking collectives, shards(): lax.psum(jnp.sum(att_total * att_total) + jnp.sum(ff_total * ff_total), (...  40.1 us
    dot_general x6, local copies, waits for them, and re-layouts, dot(): lax.dot_general(left, right, (dims, ((), ())), preferred_element_type=F32)  35.6 us
    unnamed x169, local copies, waits for them, and re-layouts  31.6 us
    all_to_all x2, starting transfers between devices, scatter_grad(): return lax.all_to_all(total.astype(BF), 'ctx', 1, 2, tiled=True).astype(F32)  25.3 us
  transfers between devices with their start and end apart: 50, of which 22 were waited for; matrix products, arithmetic and copies ran while one was open for 22% of the time, Pallas kernels for 0%

commit v1 on v0

--- a/solution.py
+++ b/solution.py
@@ -16,6 +16,35 @@
 F32 = jnp.float32
 
 
+def space_remake(local, axis_no, local_block):
+    vec_out, block_now = (local.shape[:axis_no], local.shape[axis_no + 1 :])
+    formed = local.reshape(*vec_out, local_block, -1, *block_now)
+    return jnp.moveaxis(formed, axis_no, 0)
+
+
+def mix_the_quarters(view, in_dim):
+    side_arr = list(view.shape[1:])
+    side_arr[in_dim] *= view.shape[0]
+    return jnp.moveaxis(view, 0, in_dim).reshape(side_arr)
+
+
+def zone_get(vec, mesh_dim, point, buf):
+    piece_next = lax.axis_index(mesh_dim)
+    even = lax.axis_size(mesh_dim)
+    w2, moved = (even, piece_next)
+    local_out = space_remake(vec, point, w2)
+    shelf = [local_out[moved]]
+    for k0 in range(1, w2):
+        w_next = local_out[(moved + k0) % w2]
+        z2 = lax.ppermute(
+            w_next, axis_name=mesh_dim, perm=[(src_i, (src_i + k0) % w2) for src_i in range(w2)]
+        )
+        shelf.append(z2)
+    ready = jnp.stack(shelf, axis=0)
+    local_out = ready[(moved - jnp.arange(w2)) % w2]
+    return mix_the_quarters(local_out, buf)
+
+
 def mean_spread(values):
     centre = values - jnp.mean(values, axis=-1, keepdims=True)
     spread = jnp.mean(centre * centre, axis=-1, keepdims=True)
@@ -80,7 +109,7 @@
         return total
 
     def gather_weight(shard):
-        swapped = lax.all_to_all(shard.astype(BF), "ctx", 2, 1, tiled=True)
+        swapped = zone_get(shard.astype(BF), "ctx", 2, 1)
         columns = []
         for other in range(2):
             parts = [

time: 1250 us -> 1190 us (0.952)
  waiting for transfers between devices: 598 us -> 533 us
  local copies, waits for them, and re-layouts: 154 us -> 171 us
    ppermute x24, waiting for transfers between devices: 370 us -> 275 us  [by_ctx(): lax.ppermute(block, 'ctx', [(i, (i + shift) % n_c) for i in range(n_c)])]
    ppermute x0 -> x6, waiting for transfers between devices: none -> 58.5 us  [zone_get(): lax.ppermute(w_next, axis_name=mesh_dim, perm=[(src_i, (src_i + k0) % w2)...]
    ppermute x24, starting transfers between devices: 125 us -> 94.9 us  [by_ctx(): lax.ppermute(block, 'ctx', [(i, (i + shift) % n_c) for i in range(n_c)])]
    ppermute x0 -> x6, starting transfers between devices: none -> 28.4 us  [zone_get(): lax.ppermute(w_next, axis_name=mesh_dim, perm=[(src_i, (src_i + k0) % w2)...]
    ppermute x12, waiting for transfers between devices: 222 us -> 199 us  [by_pack(): return lax.ppermute(block, ('fsdp', 'tp'), pairs)]
    unnamed x169 -> x192, local copies, waits for them, and re-layouts: 31.6 us -> 41 us
    another operation x2 -> x10, local copies, waits for them, and re-layouts: 19 us -> 26 us
    dot_general x6 -> x10, local copies, waits for them, and re-layouts: 35.6 us -> 41.6 us  [dot(): lax.dot_general(left, right, (dims, ((), ())), preferred_element_type=F32)]
  transfers between devices with their start and end apart: 50 -> 54, of which waited for: 22 -> 21; matrix products, arithmetic and copies ran while one was open for 22% -> 25% of each run, Pallas kernels for 0% -> 0%
where the time goes in v1:
time: 1190 us; the launch traced here: 1180 us
  waiting for transfers between devices  533 us (45%)
  local copies, waits for them, and re-layouts  171 us (14%)
  starting transfers between devices  164 us (14%)
  other arithmetic  139 us (12%)
  matrix products  119 us (10%)
  blocking collectives  40 us (3%)
  between operations  19.4 us (2%)
    ppermute x24, waiting for transfers between devices, by_ctx(): lax.ppermute(block, 'ctx', [(i, (i + shift) % n_c) for i in range(n_c)])  275 us
    ppermute x12, waiting for transfers between devices, by_pack(): return lax.ppermute(block, ('fsdp', 'tp'), pairs)  199 us
    dot_general x21, matrix products, dot(): lax.dot_general(left, right, (dims, ((), ())), preferred_element_type=F32)  102 us
    ppermute x24, starting transfers between devices, by_ctx(): lax.ppermute(block, 'ctx', [(i, (i + shift) % n_c) for i in range(n_c)])  94.9 us
    ppermute x6, waiting for transfers between devices, zone_get(): lax.ppermute(w_next, axis_name=mesh_dim, perm=[(src_i, (src_i + k0) % w2)...  58.5 us
    dot_general x10, local copies, waits for them, and re-layouts, dot(): lax.dot_general(left, right, (dims, ((), ())), preferred_element_type=F32)  41.6 us
    unnamed x192, local copies, waits for them, and re-layouts  41 us
    psum x1, blocking collectives, shards(): lax.psum(jnp.sum(att_total * att_total) + jnp.sum(ff_total * ff_total), (...  40 us
  transfers between devices with their start and end apart: 54, of which 21 were waited for; matrix products, arithmetic and copies ran while one was open for 25% of the time, Pallas kernels for 0%

profile of v1, /device:TPU:0, one launch (start us, length us, event | category | flops | bytes accessed | tf_op | source)
XLA Modules:
  0.0 1184.8 jit_solution(18328997110236580900)
XLA Ops:
  10.3 5.0 collective-permute-start.2
  23.9 4.1 collective-permute-done.2
  28.0 22.0 %collective-permute-start.4 = (bf16[4,256,128]{2,1,0:T(8,128)(2,1)S(1)}, bf16[4,256,128]{2,1,0:T(8,128)(2,1)S(1)}, u32[]{:S(2)}, u32[]{:S(2)}) collective-permute-start(bf16[4,256,128]{2,1,0:T(8,128)(2,1)S(1)} %bitcast.562), channel_id=1, source_target_pairs={{0,4},{4,8},{8,12},{12,0},{1,5},{5,9},{9,13},{13,1},{2,6},{6,10},{... | collective-permute-start | bytes 786440 | tf_op jit(solution)/shard_map/ppermute | solution.py:39
  50.0 22.8 %collective-permute-done.1 = bf16[128,2048]{1,0:T(8,128)(2,1)} collective-permute-done((bf16[128,2048]{1,0:T(8,128)(2,1)}, bf16[128,2048]{1,0:T(8,128)(2,1)}, u32[]{:S(2)}, u32[]{:S(2)}) %collective-permute-start.1) | collective-permute-done | bytes 524320 | tf_op jit(solution)/shard_map/ppermute | solution.py:83
  76.5 6.3 collective-permute-done.5
  91.2 19.7 %collective-permute-done.9 = bf16[4,1024,128]{2,1,0:T(8,128)(2,1)S(1)} collective-permute-done((bf16[4,1024,128]{2,1,0:T(8,128)(2,1)S(1)}, bf16[4,1024,128]{2,1,0:T(8,128)(2,1)S(1)}, u32[]{:S(2)}, u32[]{:S(2)}) %collective-permute-start.9) | collective-permute-done | bytes 1048608 | tf_op jit(solution)/shard_map/ppermute | solution.py:94
  110.9 20.5 %collective-permute-done.8 = bf16[4,1024,128]{2,1,0:T(8,128)(2,1)} collective-permute-done((bf16[4,1024,128]{2,1,0:T(8,128)(2,1)S(1)}, bf16[4,1024,128]{2,1,0:T(8,128)(2,1)}, u32[]{:S(2)}, u32[]{:S(2)}) %collective-permute-start.8) | collective-permute-done | bytes 1048608 | tf_op jit(solution)/shard_map/ppermute | solution.py:94
  150.6 7.4 fusion.136
  158.1 4.2 fusion.39
  176.7 4.6 copy.264
  194.5 5.2 convert_add_fusion.3
  200.9 20.7 %collective-permute-done.29 = bf16[128,2048]{1,0:T(8,128)(2,1)} collective-permute-done((bf16[128,2048]{1,0:T(8,128)(2,1)}, bf16[128,2048]{1,0:T(8,128)(2,1)}, u32[]{:S(2)}, u32[]{:S(2)}) %collective-permute-start.29) | collective-permute-done | bytes 524320 | tf_op jit(solution)/shard_map/ppermute | solution.py:83
  221.6 33.4 %collective-permute-start.12 = (bf16[128,2048]{1,0:T(8,128)(2,1)}, bf16[128,2048]{1,0:T(8,128)(2,1)S(1)}, u32[]{:S(2)}, u32[]{:S(2)}) collective-permute-start(bf16[128,2048]{1,0:T(8,128)(2,1)} %get-tuple-element.93), channel_id=1, source_target_pairs={{0,8},{4,12},{8,0},{12,4},{1,9},{5,13},{9,1},{13,5},{2,10},{6,14},... | collective-permute-start | bytes 1572872 | tf_op jit(solution)/shard_map/ppermute | solution.py:83
  259.2 52.3 %collective-permute-done.19 = bf16[3,256,512]{2,1,0:T(8,128)(2,1)S(1)} collective-permute-done((bf16[3,256,512]{2,1,0:T(8,128)(2,1)}, bf16[3,256,512]{2,1,0:T(8,128)(2,1)S(1)}, u32[]{:S(2)}, u32[]{:S(2)}) %collective-permute-start.19) | collective-permute-done | bytes 786464 | tf_op jit(solution)/shard_map/ppermute | solution.py:39
  314.3 4.3 gather_fusion.1
  325.9 7.7 collective-permute-done.11
  338.1 12.3 %collective-permute-done.16 = bf16[128,2048]{1,0:T(8,128)(2,1)S(1)} collective-permute-done((bf16[128,2048]{1,0:T(8,128)(2,1)S(1)}, bf16[128,2048]{1,0:T(8,128)(2,1)S(1)}, u32[]{:S(2)}, u32[]{:S(2)}) %collective-permute-start.16) | collective-permute-done | bytes 524320 | tf_op jit(solution)/shard_map/ppermute | solution.py:83
  350.4 23.3 %collective-permute-start.14 = (bf16[128,2048]{1,0:T(8,128)(2,1)S(1)}, bf16[128,2048]{1,0:T(8,128)(2,1)S(1)}, u32[]{:S(2)}, u32[]{:S(2)}) collective-permute-start(bf16[128,2048]{1,0:T(8,128)(2,1)S(1)} %fusion.79), channel_id=1, source_target_pairs={{0,4},{4,8},{8,12},{12,0},{1,5},{5,9},{9,13},{13,1},{2,6},{6,10},{... | collective-permute-start | bytes 1572872 | tf_op jit(solution)/shard_map/ppermute | solution.py:83
  378.0 8.2 reshape.641
  386.2 11.2 copy.317
  397.4 6.4 copy.300
  407.9 53.6 %collective-permute-done.22 = bf16[3,1024,512]{2,1,0:T(8,128)(2,1)} collective-permute-done((bf16[3,1024,512]{2,1,0:T(8,128)(2,1)}, bf16[3,1024,512]{2,1,0:T(8,128)(2,1)}, u32[]{:S(2)}, u32[]{:S(2)}) %collective-permute-start.22) | collective-permute-done | bytes 3145760 | tf_op jit(solution)/shard_map/ppermute | solution.py:94
  461.6 14.6 %maximum_maximum_fusion = bf16[3,2048,1024]{2,1,0:T(8,128)(2,1)S(1)} fusion(bf16[3,1024,512]{2,1,0:T(8,128)(2,1)} %collective-permute-done.23, bf16[3,1024,512]{2,1,0:T(8,128)(2,1)} %collective-permute-done.22, bf16[3,1024,512]{2,1,0:T(8,128)(2,1)} %collective-permute-done.21, bf16[3,1024,512]{2,1,0:T(8,128)(2,1)} %bitcast.71), kind=kLoop, calls=%fused_computation.4 | loop fusion | flops 50331648 | bytes 25165824 | tf_op jit(solution)/shard_map/concatenate | solution.py:119
  476.1 4.6 copy-done.14
  480.7 6.1 fusion.23
  486.8 5.3 copy.277
  494.2 8.1 fusion.22
  504.3 11.1 fusion.12
  515.3 5.3 copy.273
  520.7 5.5 copy.272
  526.2 9.3 convolution_convert_fusion.1
  535.5 13.9 %fusion.20 = f32[1024,2048]{1,0:T(8,128)} fusion(bf16[3,2048,1024]{2,1,0:T(8,128)(2,1)} %copy-done.14, f32[1024,1024]{1,0:T(8,128)S(1)} %copy-done.35, f32[1024,1024]{1,0:T(8,128)S(1)} %copy-done.31, f32[1024,1024]{1,0:T(8,128)} %copy.273), kind=kOutput, calls=%fused_computation.66 | convolution fusion | flops 4305453056 | bytes 25165824 | tf_op jit(solution)/shard_map/dot_general | solution.py:64
  549.4 11.6 add_convert_fusion.1
  564.9 6.4 copy.299
  571.3 7.3 convolution_bitcast_fusion.1
  578.6 4.6 convolution_bitcast_fusion.2
  587.8 3.8 collective-permute-start.33
  594.9 9.9 collective-permute-done.35
  604.8 22.3 %collective-permute-done.34 = bf16[128,2048]{1,0:T(8,128)(2,1)} collective-permute-done((bf16[128,2048]{1,0:T(8,128)(2,1)}, bf16[128,2048]{1,0:T(8,128)(2,1)}, u32[]{:S(2)}, u32[]{:S(2)}) %collective-permute-start.34) | collective-permute-done | bytes 524320 | tf_op jit(solution)/shard_map/ppermute | solution.py:83
  629.0 9.5 collective-permute-done.27
  638.5 32.7 %collective-permute-done.26 = bf16[128,2048]{1,0:T(8,128)(2,1)S(1)} collective-permute-done((bf16[128,2048]{1,0:T(8,128)(2,1)S(1)}, bf16[128,2048]{1,0:T(8,128)(2,1)S(1)}, u32[]{:S(2)}, u32[]{:S(2)}) %collective-permute-start.26) | collective-permute-done | bytes 524320 | tf_op jit(solution)/shard_map/ppermute | solution.py:83
  672.0 9.9 collective-permute-start.38
  684.5 7.5 convolution_bitcast_fusion
  694.4 34.8 %collective-permute-done.37 = bf16[128,2048]{1,0:T(8,128)(2,1)S(1)} collective-permute-done((bf16[128,2048]{1,0:T(8,128)(2,1)S(1)}, bf16[128,2048]{1,0:T(8,128)(2,1)S(1)}, u32[]{:S(2)}, u32[]{:S(2)}) %collective-permute-start.37) | collective-permute-done | bytes 524320 | tf_op jit(solution)/shard_map/ppermute | solution.py:83
  730.9 6.1 fusion.121
  737.0 4.0 slice_bitcast_fusion.12
  744.5 12.4 %pad_maximum_fusion = f32[3,2,1024,2,512]{4,2,3,1,0:T(8,128)} fusion(f32[1,2,1024,2,512]{4,2,3,1,0:T(8,128)} %convolution_bitcast_fusion, f32[1,2,1024,2,512]{4,2,3,1,0:T(8,128)S(1)} %convolution_bitcast_fusion.1, f32[1,2,1024,2,512]{4,2,3,1,0:T(8,128)S(1)} %convolution_bitcast_fusion.2), kind=kLoop, calls=%fused_computation.3 | loop fusion | flops 12582912 | bytes 50331648 | tf_op jit(solution)/shard_map/stack | solution.py:242
  785.8 27.3 %collective-permute-done.49 = bf16[3,1024,512]{2,1,0:T(8,128)(2,1)} collective-permute-done((bf16[3,1024,512]{2,1,0:T(8,128)(2,1)}, bf16[3,1024,512]{2,1,0:T(8,128)(2,1)}, u32[]{:S(2)}, u32[]{:S(2)}) %collective-permute-start.49) | collective-permute-done | bytes 3145760 | tf_op jit(solution)/shard_map/ppermute | solution.py:94
  813.1 78.2 %collective-permute-done.48 = bf16[3,1024,512]{2,1,0:T(8,128)(2,1)} collective-permute-done((bf16[3,1024,512]{2,1,0:T(8,128)(2,1)}, bf16[3,1024,512]{2,1,0:T(8,128)(2,1)}, u32[]{:S(2)}, u32[]{:S(2)}) %collective-permute-start.48) | collective-permute-done | bytes 3145760 | tf_op jit(solution)/shard_map/ppermute | solution.py:94
  891.4 7.2 fusion.5
  898.6 4.9 copy.304
  903.5 4.8 all-to-all-start.1
  908.4 6.4 copy.294
  939.8 52.9 %collective-permute-done.43 = bf16[128,2048]{1,0:T(8,128)(2,1)S(1)} collective-permute-done((bf16[128,2048]{1,0:T(8,128)(2,1)S(1)}, bf16[128,2048]{1,0:T(8,128)(2,1)S(1)}, u32[]{:S(2)}, u32[]{:S(2)}) %collective-permute-start.43) | collective-permute-done | bytes 524320 | tf_op jit(solution)/shard_map/ppermute | solution.py:83
  994.0 42.5 %collective-permute-done.42 = bf16[128,2048]{1,0:T(8,128)(2,1)S(1)} collective-permute-done((bf16[128,2048]{1,0:T(8,128)(2,1)S(1)}, bf16[128,2048]{1,0:T(8,128)(2,1)S(1)}, u32[]{:S(2)}, u32[]{:S(2)}) %collective-permute-start.42) | collective-permute-done | bytes 524320 | tf_op jit(solution)/shard_map/ppermute | solution.py:83
  1046.2 20.4 %all-to-all-start = ((bf16[4,1024,128]{2,0,1:T(4,128)(2,1)}), bf16[4,1024,128]{2,0,1:T(4,128)(2,1)S(1)}, u32[]{:S(2)}, u32[]{:S(2)}) async-start(bf16[4,1024,128]{2,0,1:T(4,128)(2,1)} %copy.298), calls=%async_computation | async-start | bytes 2097152 | tf_op jit(solution)/shard_map/all_to_all | solution.py:129
  1075.0 4.7 copy.307
  1079.7 6.2 slice.219
  1085.9 4.3 copy.308
  1090.2 7.1 multiply_reduce_fusion
  1104.0 40.0 %psum.7 = f32[]{:T(128)} all-reduce(f32[]{:T(128)S(6)} %add.503), channel_id=1, replica_groups=mesh['fsdp'=2,'ctx'=4,'tp'=4] {'fsdp','ctx','tp'}, use_global_device_ids=true, to_apply=%region_15.16 | all-reduce | flops 1 | bytes 8 | tf_op jit(solution)/shard_map/psum | solution.py:277
  1151.7 5.0 fusion.130
  1156.8 6.6 fusion.124
  1165.2 6.4 fusion.126
  (391 shorter events, 218.6 us)
Async XLA Ops:
  7.2 1059.4 %all-gather.3.cloned.1.call-start = ((), (), s32[]{:S(2)}) async-start(), calls=%async_computation.2 | async-start | bytes 2621440 | tf_op jit(solution)/shard_map/all_gather | solution.py:241
  8.7 324.9 %copy-start.9 = (bf16[1,128,1024]{2,1,0:T(8,128)(2,1)}, bf16[1,128,1024]{2,1,0:T(8,128)(2,1)S(1)}, u32[]{:S(2)}) copy-start(bf16[1,128,1024]{2,1,0:T(8,128)(2,1)S(1)} %get-tuple-element.96) | copy-start | bytes 786436
  8.7 324.9 %copy-start.11 = (bf16[1,128,1024]{2,1,0:T(8,128)(2,1)}, bf16[1,128,1024]{2,1,0:T(8,128)(2,1)S(1)}, u32[]{:S(2)}) copy-start(bf16[1,128,1024]{2,1,0:T(8,128)(2,1)S(1)} %get-tuple-element.97) | copy-start | bytes 786436
  10.3 17.7 %collective-permute-start.2 = (bf16[128,2048]{1,0:T(8,128)(2,1)}, bf16[128,2048]{1,0:T(8,128)(2,1)}, u32[]{:S(2)}, u32[]{:S(2)}) collective-permute-start(bf16[128,2048]{1,0:T(8,128)(2,1)} %fusion.49), channel_id=1, source_target_pairs={{0,12},{4,0},{8,4},{12,8},{1,13},{5,1},{9,5},{13,9},{2,14},{6,2},{... | collective-permute-start | bytes 1572872 | tf_op jit(solution)/shard_map/ppermute | solution.py:83
  15.3 57.5 %collective-permute-start.1 = (bf16[128,2048]{1,0:T(8,128)(2,1)}, bf16[128,2048]{1,0:T(8,128)(2,1)}, u32[]{:S(2)}, u32[]{:S(2)}) collective-permute-start(bf16[128,2048]{1,0:T(8,128)(2,1)} %fusion.49), channel_id=1, source_target_pairs={{0,8},{4,12},{8,0},{12,4},{1,9},{5,13},{9,1},{13,5},{2,10},{6,14},... | collective-permute-start | bytes 1572872 | tf_op jit(solution)/shard_map/ppermute | solution.py:83
  15.3 57.5 %collective-permute-start = (bf16[128,2048]{1,0:T(8,128)(2,1)}, bf16[128,2048]{1,0:T(8,128)(2,1)}, u32[]{:S(2)}, u32[]{:S(2)}) collective-permute-start(bf16[128,2048]{1,0:T(8,128)(2,1)} %fusion.49), channel_id=1, source_target_pairs={{0,4},{4,8},{8,12},{12,0},{1,5},{5,9},{9,13},{13,1},{2,6},{6,10},{... | collective-permute-start | bytes 1572872 | tf_op jit(solution)/shard_map/ppermute | solution.py:83
  18.1 58.4 %collective-permute-start.6 = (bf16[4,256,128]{2,1,0:T(8,128)(2,1)S(1)}, bf16[4,256,128]{2,1,0:T(8,128)(2,1)S(1)}, u32[]{:S(2)}, u32[]{:S(2)}) collective-permute-start(bf16[4,256,128]{2,1,0:T(8,128)(2,1)S(1)} %bitcast.560), channel_id=1, source_target_pairs={{0,12},{4,0},{8,4},{12,8},{1,13},{5,1},{9,5},{13,9},{2,14},{6,2},{... | collective-permute-start | bytes 786440 | tf_op jit(solution)/shard_map/ppermute | solution.py:39
  21.2 61.6 %collective-permute-start.5 = (bf16[4,256,128]{2,1,0:T(8,128)(2,1)S(1)}, bf16[4,256,128]{2,1,0:T(8,128)(2,1)S(1)}, u32[]{:S(2)}, u32[]{:S(2)}) collective-permute-start(bf16[4,256,128]{2,1,0:T(8,128)(2,1)S(1)} %bitcast.561), channel_id=1, source_target_pairs={{0,8},{4,12},{8,0},{12,4},{1,9},{5,13},{9,1},{13,5},{2,10},{6,14},... | collective-permute-start | bytes 786440 | tf_op jit(solution)/shard_map/ppermute | solution.py:39
  28.0 54.8 %collective-permute-start.4 = (bf16[4,256,128]{2,1,0:T(8,128)(2,1)S(1)}, bf16[4,256,128]{2,1,0:T(8,128)(2,1)S(1)}, u32[]{:S(2)}, u32[]{:S(2)}) collective-permute-start(bf16[4,256,128]{2,1,0:T(8,128)(2,1)S(1)} %bitcast.562), channel_id=1, source_target_pairs={{0,4},{4,8},{8,12},{12,0},{1,5},{5,9},{9,13},{13,1},{2,6},{6,10},{... | collective-permute-start | bytes 786440 | tf_op jit(solution)/shard_map/ppermute | solution.py:39
  76.5 65.0 %collective-permute-start.3 = (bf16[4,128,2048]{2,1,0:T(8,128)(2,1)}, bf16[4,128,2048]{2,1,0:T(8,128)(2,1)}, u32[]{:S(2)}, u32[]{:S(2)}) collective-permute-start(bf16[4,128,2048]{2,1,0:T(8,128)(2,1)} %get-tuple-element.95), channel_id=1, source_target_pairs={{0,1},{1,0},{2,3},{3,2},{4,5},{5,4},{6,7},{7,6},{8,9},{9,8},{10,11... | collective-permute-start | bytes 6291464 | tf_op jit(solution)/shard_map/ppermute | solution.py:86
  83.8 27.1 %collective-permute-start.9 = (bf16[4,1024,128]{2,1,0:T(8,128)(2,1)S(1)}, bf16[4,1024,128]{2,1,0:T(8,128)(2,1)S(1)}, u32[]{:S(2)}, u32[]{:S(2)}) collective-permute-start(bf16[4,1024,128]{2,1,0:T(8,128)(2,1)S(1)} %bitcast.532), channel_id=1, source_target_pairs={{0,18},{1,19},{2,16},{3,17},{16,2},{17,3},{18,0},{19,1},{4,22},{5,... | collective-permute-start | bytes 3145736 | tf_op jit(solution)/shard_map/ppermute | solution.py:94
  86.3 45.1 %collective-permute-start.8 = (bf16[4,1024,128]{2,1,0:T(8,128)(2,1)S(1)}, bf16[4,1024,128]{2,1,0:T(8,128)(2,1)}, u32[]{:S(2)}, u32[]{:S(2)}) collective-permute-start(bf16[4,1024,128]{2,1,0:T(8,128)(2,1)S(1)} %bitcast.533), channel_id=1, source_target_pairs={{0,2},{1,3},{2,0},{3,1},{16,18},{17,19},{18,16},{19,17},{4,6},{5,7... | collective-permute-start | bytes 3145736 | tf_op jit(solution)/shard_map/ppermute | solution.py:94
  86.8 44.6 %collective-permute-start.7 = (bf16[4,1024,128]{2,1,0:T(8,128)(2,1)S(1)}, bf16[4,1024,128]{2,1,0:T(8,128)(2,1)}, u32[]{:S(2)}, u32[]{:S(2)}) collective-permute-start(bf16[4,1024,128]{2,1,0:T(8,128)(2,1)S(1)} %bitcast.534), channel_id=1, source_target_pairs={{0,16},{1,17},{2,18},{3,19},{16,0},{17,1},{18,2},{19,3},{4,20},{5,... | collective-permute-start | bytes 3145736 | tf_op jit(solution)/shard_map/ppermute | solution.py:94
  168.5 25.4 %collective-permute-start.10 = (bf16[4,128,2048]{2,1,0:T(8,128)(2,1)}, bf16[4,128,2048]{2,1,0:T(8,128)(2,1)}, u32[]{:S(2)}, u32[]{:S(2)}) collective-permute-start(bf16[4,128,2048]{2,1,0:T(8,128)(2,1)} %slice_bitcast_fusion.20), channel_id=1, source_target_pairs={{0,1},{1,0},{2,3},{3,2},{4,5},{5,4},{6,7},{7,6},{8,9},{9,8},{10,11... | collective-permute-start | bytes 6291464 | tf_op jit(solution)/shard_map/ppermute | solution.py:86
  171.6 22.3 %collective-permute-start.30 = (bf16[128,2048]{1,0:T(8,128)(2,1)}, bf16[128,2048]{1,0:T(8,128)(2,1)}, u32[]{:S(2)}, u32[]{:S(2)}) collective-permute-start(bf16[128,2048]{1,0:T(8,128)(2,1)} %get-tuple-element.116), channel_id=1, source_target_pairs={{0,12},{4,0},{8,4},{12,8},{1,13},{5,1},{9,5},{13,9},{2,14},{6,2},{... | collective-permute-start | bytes 1572872 | tf_op jit(solution)/shard_map/ppermute | solution.py:83
  171.6 49.9 %collective-permute-start.29 = (bf16[128,2048]{1,0:T(8,128)(2,1)}, bf16[128,2048]{1,0:T(8,128)(2,1)}, u32[]{:S(2)}, u32[]{:S(2)}) collective-permute-start(bf16[128,2048]{1,0:T(8,128)(2,1)} %get-tuple-element.116), channel_id=1, source_target_pairs={{0,8},{4,12},{8,0},{12,4},{1,9},{5,13},{9,1},{13,5},{2,10},{6,14},... | collective-permute-start | bytes 1572872 | tf_op jit(solution)/shard_map/ppermute | solution.py:83
  174.7 46.8 %collective-permute-start.28 = (bf16[128,2048]{1,0:T(8,128)(2,1)}, bf16[128,2048]{1,0:T(8,128)(2,1)}, u32[]{:S(2)}, u32[]{:S(2)}) collective-permute-start(bf16[128,2048]{1,0:T(8,128)(2,1)} %get-tuple-element.116), channel_id=1, source_target_pairs={{0,4},{4,8},{8,12},{12,0},{1,5},{5,9},{9,13},{13,1},{2,6},{6,10},{... | collective-permute-start | bytes 1572872 | tf_op jit(solution)/shard_map/ppermute | solution.py:83
  188.3 66.7 %collective-permute-start.20 = (bf16[3,256,512]{2,1,0:T(8,128)(2,1)}, bf16[3,256,512]{2,1,0:T(8,128)(2,1)}, u32[]{:S(2)}, u32[]{:S(2)}) collective-permute-start(bf16[3,256,512]{2,1,0:T(8,128)(2,1)} %bitcast.68), channel_id=1, source_target_pairs={{0,12},{4,0},{8,4},{12,8},{1,13},{5,1},{9,5},{13,9},{2,14},{6,2},{... | collective-permute-start | bytes 2359304 | tf_op jit(solution)/shard_map/ppermute | solution.py:39
  193.9 117.5 %collective-permute-start.19 = (bf16[3,256,512]{2,1,0:T(8,128)(2,1)}, bf16[3,256,512]{2,1,0:T(8,128)(2,1)S(1)}, u32[]{:S(2)}, u32[]{:S(2)}) collective-permute-start(bf16[3,256,512]{2,1,0:T(8,128)(2,1)} %bitcast.552), channel_id=1, source_target_pairs={{0,8},{4,12},{8,0},{12,4},{1,9},{5,13},{9,1},{13,5},{2,10},{6,14},... | collective-permute-start | bytes 2359304 | tf_op jit(solution)/shard_map/ppermute | solution.py:39
  194.0 61.5 %copy-start.44 = (bf16[1,128,2048]{2,1,0:T(8,128)(2,1)S(1)}, bf16[1,128,2048]{2,1,0:T(8,128)(2,1)}, u32[]{:S(2)}) copy-start(bf16[1,128,2048]{2,1,0:T(8,128)(2,1)} %get-tuple-element.115) | copy-start | bytes 1572868
  194.0 117.4 %collective-permute-start.18 = (bf16[3,256,512]{2,1,0:T(8,128)(2,1)}, bf16[3,256,512]{2,1,0:T(8,128)(2,1)S(1)}, u32[]{:S(2)}, u32[]{:S(2)}) collective-permute-start(bf16[3,256,512]{2,1,0:T(8,128)(2,1)} %bitcast.551), channel_id=1, source_target_pairs={{0,4},{4,8},{8,12},{12,0},{1,5},{5,9},{9,13},{13,1},{2,6},{6,10},{... | collective-permute-start | bytes 2359304 | tf_op jit(solution)/shard_map/ppermute | solution.py:39
  221.5 102.5 %collective-permute-start.13 = (bf16[128,2048]{1,0:T(8,128)(2,1)}, bf16[128,2048]{1,0:T(8,128)(2,1)S(1)}, u32[]{:S(2)}, u32[]{:S(2)}) collective-permute-start(bf16[128,2048]{1,0:T(8,128)(2,1)} %get-tuple-element.92), channel_id=1, source_target_pairs={{0,4},{4,8},{8,12},{12,0},{1,5},{5,9},{9,13},{13,1},{2,6},{6,10},{... | collective-permute-start | bytes 1572872 | tf_op jit(solution)/shard_map/ppermute | solution.py:83
  221.6 103.8 %collective-permute-start.12 = (bf16[128,2048]{1,0:T(8,128)(2,1)}, bf16[128,2048]{1,0:T(8,128)(2,1)S(1)}, u32[]{:S(2)}, u32[]{:S(2)}) collective-permute-start(bf16[128,2048]{1,0:T(8,128)(2,1)} %get-tuple-element.93), channel_id=1, source_target_pairs={{0,8},{4,12},{8,0},{12,4},{1,9},{5,13},{9,1},{13,5},{2,10},{6,14},... | collective-permute-start | bytes 1572872 | tf_op jit(solution)/shard_map/ppermute | solution.py:83
  255.0 78.6 %collective-permute-start.11 = (bf16[128,2048]{1,0:T(8,128)(2,1)}, bf16[128,2048]{1,0:T(8,128)(2,1)S(1)}, u32[]{:S(2)}, u32[]{:S(2)}) collective-permute-start(bf16[128,2048]{1,0:T(8,128)(2,1)} %get-tuple-element.91), channel_id=1, source_target_pairs={{0,12},{4,0},{8,4},{12,8},{1,13},{5,1},{9,5},{13,9},{2,14},{6,2},{... | collective-permute-start | bytes 1572872 | tf_op jit(solution)/shard_map/ppermute | solution.py:83
  311.4 26.7 %collective-permute-start.31 = (bf16[4,128,2048]{2,1,0:T(8,128)(2,1)}, bf16[4,128,2048]{2,1,0:T(8,128)(2,1)}, u32[]{:S(2)}, u32[]{:S(2)}) collective-permute-start(bf16[4,128,2048]{2,1,0:T(8,128)(2,1)} %get-tuple-element.83), channel_id=1, source_target_pairs={{0,1},{1,0},{2,3},{3,2},{4,5},{5,4},{6,7},{7,6},{8,9},{9,8},{10,11... | collective-permute-start | bytes 6291464 | tf_op jit(solution)/shard_map/ppermute | solution.py:86
  322.4 85.5 %collective-permute-start.23 = (bf16[3,1024,512]{2,1,0:T(8,128)(2,1)}, bf16[3,1024,512]{2,1,0:T(8,128)(2,1)}, u32[]{:S(2)}, u32[]{:S(2)}) collective-permute-start(bf16[3,1024,512]{2,1,0:T(8,128)(2,1)} %bitcast.71), channel_id=1, source_target_pairs={{0,18},{1,19},{2,16},{3,17},{16,2},{17,3},{18,0},{19,1},{4,22},{5,... | collective-permute-start | bytes 9437192 | tf_op jit(solution)/shard_map/ppermute | solution.py:94
  324.1 137.5 %collective-permute-start.22 = (bf16[3,1024,512]{2,1,0:T(8,128)(2,1)}, bf16[3,1024,512]{2,1,0:T(8,128)(2,1)}, u32[]{:S(2)}, u32[]{:S(2)}) collective-permute-start(bf16[3,1024,512]{2,1,0:T(8,128)(2,1)} %bitcast.71), channel_id=1, source_target_pairs={{0,2},{1,3},{2,0},{3,1},{16,18},{17,19},{18,16},{19,17},{4,6},{5,7... | collective-permute-start | bytes 9437192 | tf_op jit(solution)/shard_map/ppermute | solution.py:94
  325.4 136.2 %collective-permute-start.21 = (bf16[3,1024,512]{2,1,0:T(8,128)(2,1)}, bf16[3,1024,512]{2,1,0:T(8,128)(2,1)}, u32[]{:S(2)}, u32[]{:S(2)}) collective-permute-start(bf16[3,1024,512]{2,1,0:T(8,128)(2,1)} %bitcast.71), channel_id=1, source_target_pairs={{0,16},{1,17},{2,18},{3,19},{16,0},{17,1},{18,2},{19,3},{4,20},{5,... | collective-permute-start | bytes 9437192 | tf_op jit(solution)/shard_map/ppermute | solution.py:94
  335.8 14.6 %collective-permute-start.16 = (bf16[128,2048]{1,0:T(8,128)(2,1)S(1)}, bf16[128,2048]{1,0:T(8,128)(2,1)S(1)}, u32[]{:S(2)}, u32[]{:S(2)}) collective-permute-start(bf16[128,2048]{1,0:T(8,128)(2,1)S(1)} %fusion.79), channel_id=1, source_target_pairs={{0,12},{4,0},{8,4},{12,8},{1,13},{5,1},{9,5},{13,9},{2,14},{6,2},{... | collective-permute-start | bytes 1572872 | tf_op jit(solution)/shard_map/ppermute | solution.py:83
  338.1 65.8 %collective-permute-start.15 = (bf16[128,2048]{1,0:T(8,128)(2,1)S(1)}, bf16[128,2048]{1,0:T(8,128)(2,1)S(1)}, u32[]{:S(2)}, u32[]{:S(2)}) collective-permute-start(bf16[128,2048]{1,0:T(8,128)(2,1)S(1)} %fusion.79), channel_id=1, source_target_pairs={{0,8},{4,12},{8,0},{12,4},{1,9},{5,13},{9,1},{13,5},{2,10},{6,14},... | collective-permute-start | bytes 1572872 | tf_op jit(solution)/shard_map/ppermute | solution.py:83
  350.4 53.5 %collective-permute-start.14 = (bf16[128,2048]{1,0:T(8,128)(2,1)S(1)}, bf16[128,2048]{1,0:T(8,128)(2,1)S(1)}, u32[]{:S(2)}, u32[]{:S(2)}) collective-permute-start(bf16[128,2048]{1,0:T(8,128)(2,1)S(1)} %fusion.79), channel_id=1, source_target_pairs={{0,4},{4,8},{8,12},{12,0},{1,5},{5,9},{9,13},{13,1},{2,6},{6,10},{... | collective-permute-start | bytes 1572872 | tf_op jit(solution)/shard_map/ppermute | solution.py:83
  407.9 72.8 %copy-start.7 = (bf16[4,2,128,2048]{3,2,1,0:T(8,128)(2,1)S(1)}, bf16[4,2,128,2048]{3,2,1,0:T(8,128)(2,1)}, u32[]{:S(2)}) copy-start(bf16[4,2,128,2048]{3,2,1,0:T(8,128)(2,1)} %copy.276) | copy-start | bytes 12582916
  407.9 84.2 %collective-permute-start.17 = (bf16[4,128,2048]{2,1,0:T(8,128)(2,1)}, bf16[4,128,2048]{2,1,0:T(8,128)(2,1)}, u32[]{:S(2)}, u32[]{:S(2)}) collective-permute-start(bf16[4,128,2048]{2,1,0:T(8,128)(2,1)} %get-tuple-element.90), channel_id=1, source_target_pairs={{0,1},{1,0},{2,3},{3,2},{4,5},{5,4},{6,7},{7,6},{8,9},{9,8},{10,11... | collective-permute-start | bytes 6291464 | tf_op jit(solution)/shard_map/ppermute | solution.py:86
  562.8 20.5 %collective-permute-start.32 = (bf16[4,128,2048]{2,1,0:T(8,128)(2,1)}, bf16[4,128,2048]{2,1,0:T(8,128)(2,1)}, u32[]{:S(2)}, u32[]{:S(2)}) collective-permute-start(bf16[4,128,2048]{2,1,0:T(8,128)(2,1)} %slice_bitcast_fusion.16), channel_id=1, source_target_pairs={{0,1},{1,0},{2,3},{3,2},{4,5},{5,4},{6,7},{7,6},{8,9},{9,8},{10,11... | collective-permute-start | bytes 6291464 | tf_op jit(solution)/shard_map/ppermute | solution.py:86
  564.5 27.1 %collective-permute-start.24 = (bf16[4,128,2048]{2,1,0:T(8,128)(2,1)}, bf16[4,128,2048]{2,1,0:T(8,128)(2,1)S(1)}, u32[]{:S(2)}, u32[]{:S(2)}) collective-permute-start(bf16[4,128,2048]{2,1,0:T(8,128)(2,1)} %slice_bitcast_fusion.18), channel_id=1, source_target_pairs={{0,1},{1,0},{2,3},{3,2},{4,5},{5,4},{6,7},{7,6},{8,9},{9,8},{10,11... | collective-permute-start | bytes 6291464 | tf_op jit(solution)/shard_map/ppermute | solution.py:86
  587.8 17.0 %collective-permute-start.35 = (bf16[128,2048]{1,0:T(8,128)(2,1)}, bf16[128,2048]{1,0:T(8,128)(2,1)}, u32[]{:S(2)}, u32[]{:S(2)}) collective-permute-start(bf16[128,2048]{1,0:T(8,128)(2,1)} %get-tuple-element.80), channel_id=1, source_target_pairs={{0,4},{4,8},{8,12},{12,0},{1,5},{5,9},{9,13},{13,1},{2,6},{6,10},{... | collective-permute-start | bytes 1572872 | tf_op jit(solution)/shard_map/ppermute | solution.py:83
  587.8 39.3 %collective-permute-start.34 = (bf16[128,2048]{1,0:T(8,128)(2,1)}, bf16[128,2048]{1,0:T(8,128)(2,1)}, u32[]{:S(2)}, u32[]{:S(2)}) collective-permute-start(bf16[128,2048]{1,0:T(8,128)(2,1)} %get-tuple-element.81), channel_id=1, source_target_pairs={{0,8},{4,12},{8,0},{12,4},{1,9},{5,13},{9,1},{13,5},{2,10},{6,14},... | collective-permute-start | bytes 1572872 | tf_op jit(solution)/shard_map/ppermute | solution.py:83
  587.8 39.3 %collective-permute-start.33 = (bf16[128,2048]{1,0:T(8,128)(2,1)}, bf16[128,2048]{1,0:T(8,128)(2,1)}, u32[]{:S(2)}, u32[]{:S(2)}) collective-permute-start(bf16[128,2048]{1,0:T(8,128)(2,1)} %get-tuple-element.79), channel_id=1, source_target_pairs={{0,12},{4,0},{8,4},{12,8},{1,13},{5,1},{9,5},{13,9},{2,14},{6,2},{... | collective-permute-start | bytes 1572872 | tf_op jit(solution)/shard_map/ppermute | solution.py:83
  592.5 78.6 %copy-start.40 = (bf16[128,1024]{1,0:T(8,128)(2,1)S(1)}, bf16[128,1024]{1,0:T(8,128)(2,1)}, u32[]{:S(2)}) copy-start(bf16[128,1024]{1,0:T(8,128)(2,1)} %copy-done.39) | copy-start | bytes 786436
  592.6 78.6 %copy-start.42 = (bf16[128,1024]{1,0:T(8,128)(2,1)S(1)}, bf16[128,1024]{1,0:T(8,128)(2,1)}, u32[]{:S(2)}) copy-start(bf16[128,1024]{1,0:T(8,128)(2,1)} %copy-done.41) | copy-start | bytes 786436
  592.7 45.7 %collective-permute-start.27 = (bf16[128,2048]{1,0:T(8,128)(2,1)S(1)}, bf16[128,2048]{1,0:T(8,128)(2,1)S(1)}, u32[]{:S(2)}, u32[]{:S(2)}) collective-permute-start(bf16[128,2048]{1,0:T(8,128)(2,1)S(1)} %get-tuple-element.87), channel_id=1, source_target_pairs={{0,4},{4,8},{8,12},{12,0},{1,5},{5,9},{9,13},{13,1},{2,6},{6,10},{... | collective-permute-start | bytes 1572872 | tf_op jit(solution)/shard_map/ppermute | solution.py:83
  593.4 77.8 %collective-permute-start.26 = (bf16[128,2048]{1,0:T(8,128)(2,1)S(1)}, bf16[128,2048]{1,0:T(8,128)(2,1)S(1)}, u32[]{:S(2)}, u32[]{:S(2)}) collective-permute-start(bf16[128,2048]{1,0:T(8,128)(2,1)S(1)} %get-tuple-element.88), channel_id=1, source_target_pairs={{0,8},{4,12},{8,0},{12,4},{1,9},{5,13},{9,1},{13,5},{2,10},{6,14},... | collective-permute-start | bytes 1572872 | tf_op jit(solution)/shard_map/ppermute | solution.py:83
  604.8 66.4 %collective-permute-start.25 = (bf16[128,2048]{1,0:T(8,128)(2,1)S(1)}, bf16[128,2048]{1,0:T(8,128)(2,1)S(1)}, u32[]{:S(2)}, u32[]{:S(2)}) collective-permute-start(bf16[128,2048]{1,0:T(8,128)(2,1)S(1)} %get-tuple-element.86), channel_id=1, source_target_pairs={{0,12},{4,0},{8,4},{12,8},{1,13},{5,1},{9,5},{13,9},{2,14},{6,2},{... | collective-permute-start | bytes 1572872 | tf_op jit(solution)/shard_map/ppermute | solution.py:83
  672.0 22.4 %collective-permute-start.38 = (bf16[128,2048]{1,0:T(8,128)(2,1)S(1)}, bf16[128,2048]{1,0:T(8,128)(2,1)S(1)}, u32[]{:S(2)}, u32[]{:S(2)}) collective-permute-start(bf16[128,2048]{1,0:T(8,128)(2,1)S(1)} %get-tuple-element.45), channel_id=1, source_target_pairs={{0,12},{4,0},{8,4},{12,8},{1,13},{5,1},{9,5},{13,9},{2,14},{6,2},{... | collective-permute-start | bytes 1572872 | tf_op jit(solution)/shard_map/ppermute | solution.py:83
  682.0 47.3 %collective-permute-start.37 = (bf16[128,2048]{1,0:T(8,128)(2,1)S(1)}, bf16[128,2048]{1,0:T(8,128)(2,1)S(1)}, u32[]{:S(2)}, u32[]{:S(2)}) collective-permute-start(bf16[128,2048]{1,0:T(8,128)(2,1)S(1)} %get-tuple-element.45), channel_id=1, source_target_pairs={{0,8},{4,12},{8,0},{12,4},{1,9},{5,13},{9,1},{13,5},{2,10},{6,14},... | collective-permute-start | bytes 1572872 | tf_op jit(solution)/shard_map/ppermute | solution.py:83
  684.5 44.8 %collective-permute-start.36 = (bf16[128,2048]{1,0:T(8,128)(2,1)S(1)}, bf16[128,2048]{1,0:T(8,128)(2,1)S(1)}, u32[]{:S(2)}, u32[]{:S(2)}) collective-permute-start(bf16[128,2048]{1,0:T(8,128)(2,1)S(1)} %get-tuple-element.45), channel_id=1, source_target_pairs={{0,4},{4,8},{8,12},{12,0},{1,5},{5,9},{9,13},{13,1},{2,6},{6,10},{... | collective-permute-start | bytes 1572872 | tf_op jit(solution)/shard_map/ppermute | solution.py:83
  730.9 26.9 %collective-permute-start.39 = (bf16[4,128,2048]{2,1,0:T(8,128)(2,1)}, bf16[4,128,2048]{2,1,0:T(8,128)(2,1)}, u32[]{:S(2)}, u32[]{:S(2)}) collective-permute-start(bf16[4,128,2048]{2,1,0:T(8,128)(2,1)} %get-tuple-element.78), channel_id=1, source_target_pairs={{0,1},{1,0},{2,3},{3,2},{4,5},{5,4},{6,7},{7,6},{8,9},{9,8},{10,11... | collective-permute-start | bytes 6291464 | tf_op jit(solution)/shard_map/ppermute | solution.py:86
  741.0 72.2 %collective-permute-start.49 = (bf16[3,1024,512]{2,1,0:T(8,128)(2,1)}, bf16[3,1024,512]{2,1,0:T(8,128)(2,1)}, u32[]{:S(2)}, u32[]{:S(2)}) collective-permute-start(bf16[3,1024,512]{2,1,0:T(8,128)(2,1)} %get-tuple-element.51), channel_id=1, source_target_pairs={{0,18},{1,19},{2,16},{3,17},{16,2},{17,3},{18,0},{19,1},{4,22},{5,... | collective-permute-start | bytes 9437192 | tf_op jit(solution)/shard_map/ppermute | solution.py:94
  742.6 148.8 %collective-permute-start.48 = (bf16[3,1024,512]{2,1,0:T(8,128)(2,1)}, bf16[3,1024,512]{2,1,0:T(8,128)(2,1)}, u32[]{:S(2)}, u32[]{:S(2)}) collective-permute-start(bf16[3,1024,512]{2,1,0:T(8,128)(2,1)} %get-tuple-element.52), channel_id=1, source_target_pairs={{0,2},{1,3},{2,0},{3,1},{16,18},{17,19},{18,16},{19,17},{4,6},{5,7... | collective-permute-start | bytes 9437192 | tf_op jit(solution)/shard_map/ppermute | solution.py:94
  743.8 147.6 %collective-permute-start.47 = (bf16[3,1024,512]{2,1,0:T(8,128)(2,1)}, bf16[3,1024,512]{2,1,0:T(8,128)(2,1)}, u32[]{:S(2)}, u32[]{:S(2)}) collective-permute-start(bf16[3,1024,512]{2,1,0:T(8,128)(2,1)} %get-tuple-element.50), channel_id=1, source_target_pairs={{0,16},{1,17},{2,18},{3,19},{16,0},{17,1},{18,2},{19,3},{4,20},{5,... | collective-permute-start | bytes 9437192 | tf_op jit(solution)/shard_map/ppermute | solution.py:94
  785.8 139.2 %collective-permute-start.40 = (bf16[4,128,2048]{2,1,0:T(8,128)(2,1)}, bf16[4,128,2048]{2,1,0:T(8,128)(2,1)}, u32[]{:S(2)}, u32[]{:S(2)}) collective-permute-start(bf16[4,128,2048]{2,1,0:T(8,128)(2,1)} %slice_bitcast_fusion.14), channel_id=1, source_target_pairs={{0,1},{1,0},{2,3},{3,2},{4,5},{5,4},{6,7},{7,6},{8,9},{9,8},{10,11... | collective-permute-start | bytes 6291464 | tf_op jit(solution)/shard_map/ppermute | solution.py:86
  903.5 142.6 %all-to-all-start.1 = ((bf16[3,1024,512]{2,0,1:T(4,128)(2,1)}), bf16[3,1024,512]{2,0,1:T(4,128)(2,1)}, u32[]{:S(2)}, u32[]{:S(2)}) async-start(bf16[3,1024,512]{2,0,1:T(4,128)(2,1)} %copy.304), calls=%async_computation.1 | async-start | bytes 8388608 | tf_op jit(solution)/shard_map/all_to_all | solution.py:129
  908.4 263.2 %all-gather.5.cloned.1.call-start = ((), (), s32[]{:S(2)}) async-start(), calls=%async_computation.3 | async-start | bytes 5242880 | tf_op jit(solution)/shard_map/all_gather | solution.py:271
  928.4 64.2 %collective-permute-start.43 = (bf16[128,2048]{1,0:T(8,128)(2,1)S(1)}, bf16[128,2048]{1,0:T(8,128)(2,1)S(1)}, u32[]{:S(2)}, u32[]{:S(2)}) collective-permute-start(bf16[128,2048]{1,0:T(8,128)(2,1)S(1)} %get-tuple-element.75), channel_id=1, source_target_pairs={{0,4},{4,8},{8,12},{12,0},{1,5},{5,9},{9,13},{13,1},{2,6},{6,10},{... | collective-permute-start | bytes 1572872 | tf_op jit(solution)/shard_map/ppermute | solution.py:83
  930.4 106.1 %collective-permute-start.42 = (bf16[128,2048]{1,0:T(8,128)(2,1)S(1)}, bf16[128,2048]{1,0:T(8,128)(2,1)S(1)}, u32[]{:S(2)}, u32[]{:S(2)}) collective-permute-start(bf16[128,2048]{1,0:T(8,128)(2,1)S(1)} %get-tuple-element.76), channel_id=1, source_target_pairs={{0,8},{4,12},{8,0},{12,4},{1,9},{5,13},{9,1},{13,5},{2,10},{6,14},... | collective-permute-start | bytes 1572872 | tf_op jit(solution)/shard_map/ppermute | solution.py:83
  932.8 103.8 %collective-permute-start.41 = (bf16[128,2048]{1,0:T(8,128)(2,1)S(1)}, bf16[128,2048]{1,0:T(8,128)(2,1)S(1)}, u32[]{:S(2)}, u32[]{:S(2)}) collective-permute-start(bf16[128,2048]{1,0:T(8,128)(2,1)S(1)} %get-tuple-element.74), channel_id=1, source_target_pairs={{0,12},{4,0},{8,4},{12,8},{1,13},{5,1},{9,5},{13,9},{2,14},{6,2},{... | collective-permute-start | bytes 1572872 | tf_op jit(solution)/shard_map/ppermute | solution.py:83
  935.2 101.4 %copy-start.10 = (bf16[1,128,1024]{2,1,0:T(8,128)(2,1)S(1)}, bf16[1,128,1024]{2,1,0:T(8,128)(2,1)}, u32[]{:S(2)}) copy-start(bf16[1,128,1024]{2,1,0:T(8,128)(2,1)} %copy-done.9) | copy-start | bytes 786436
  935.2 101.4 %copy-start.12 = (bf16[1,128,1024]{2,1,0:T(8,128)(2,1)S(1)}, bf16[1,128,1024]{2,1,0:T(8,128)(2,1)}, u32[]{:S(2)}) copy-start(bf16[1,128,1024]{2,1,0:T(8,128)(2,1)} %copy-done.11) | copy-start | bytes 786436
  935.2 101.3 %copy-start.74 = (f32[128]{0:T(128)S(1)}, f32[128]{0:T(128)}, u32[]{:S(2)}) copy-start(f32[128]{0:T(128)} %copy-done.73) | copy-start | bytes 1540
  935.2 101.3 %copy-start.78 = (f32[128]{0:T(128)S(1)}, f32[128]{0:T(128)}, u32[]{:S(2)}) copy-start(f32[128]{0:T(128)} %copy-done.77) | copy-start | bytes 1540
  937.0 105.0 %collective-permute-start.46 = (bf16[4,1024,128]{2,1,0:T(8,128)(2,1)}, bf16[4,1024,128]{2,1,0:T(8,128)(2,1)}, u32[]{:S(2)}, u32[]{:S(2)}) collective-permute-start(bf16[4,1024,128]{2,1,0:T(8,128)(2,1)} %get-tuple-element.65), channel_id=1, source_target_pairs={{0,18},{1,19},{2,16},{3,17},{16,2},{17,3},{18,0},{19,1},{4,22},{5,... | collective-permute-start | bytes 3145736 | tf_op jit(solution)/shard_map/ppermute | solution.py:94
  938.5 103.5 %collective-permute-start.45 = (bf16[4,1024,128]{2,1,0:T(8,128)(2,1)}, bf16[4,1024,128]{2,1,0:T(8,128)(2,1)}, u32[]{:S(2)}, u32[]{:S(2)}) collective-permute-start(bf16[4,1024,128]{2,1,0:T(8,128)(2,1)} %get-tuple-element.66), channel_id=1, source_target_pairs={{0,2},{1,3},{2,0},{3,1},{16,18},{17,19},{18,16},{19,17},{4,6},{5,7... | collective-permute-start | bytes 3145736 | tf_op jit(solution)/shard_map/ppermute | solution.py:94
  992.7 49.4 %collective-permute-start.44 = (bf16[4,1024,128]{2,1,0:T(8,128)(2,1)}, bf16[4,1024,128]{2,1,0:T(8,128)(2,1)}, u32[]{:S(2)}, u32[]{:S(2)}) collective-permute-start(bf16[4,1024,128]{2,1,0:T(8,128)(2,1)} %get-tuple-element.64), channel_id=1, source_target_pairs={{0,16},{1,17},{2,18},{3,19},{16,0},{17,1},{18,2},{19,3},{4,20},{5,... | collective-permute-start | bytes 3145736 | tf_op jit(solution)/shard_map/ppermute | solution.py:94
  1046.2 51.1 %all-to-all-start = ((bf16[4,1024,128]{2,0,1:T(4,128)(2,1)}), bf16[4,1024,128]{2,0,1:T(4,128)(2,1)S(1)}, u32[]{:S(2)}, u32[]{:S(2)}) async-start(bf16[4,1024,128]{2,0,1:T(4,128)(2,1)} %copy.298), calls=%async_computation | async-start | bytes 2097152 | tf_op jit(solution)/shard_map/all_to_all | solution.py:129
  (79 other events, 649.8 us)
Sparse Core Ops, SparseCore 0:
  757.9 78.7 all-gather.2
  1039.0 43.0 all-gather.4
